TPU v7x, 32 devices: a whole 2x2x4 slice. The times are simulated.
32 devices in a mesh: gx: 8 (over z, y), gy: 4 (over x, core).
Axes of the slice: x: 2, y: 2, z: 4, core: 2. Of those that a mesh axis runs over, the one named last changes fastest.
Arguments:
- right_side: float32 [64, 128, 128], P('gy', 'gx'), may hold values from -6 to 9
- diagonal: float32 [64, 128, 128], P('gy', 'gx'), may hold values from 0.02 to 0.5
- horizontal: float32 [64, 128, 128], P('gy', 'gx'), may hold values from 0.1 to 1
- vertical: float32 [128], replicated, may hold values from 0.2 to 2
- precond: float32 [2, 128, 128], replicated, may hold values from -4 to 4
- edge_rows: int32 [2, 64], replicated, may hold values from 0 to 63, as said below
Outputs:
- solution_field: float32 [64, 128, 128], P('gy', 'gx')
- residual: float32 [64, 128, 128], P('gy', 'gx')
- residual_sq: float32 [3], replicated
Inputs may be any that keep to these rules, and one draw needn't show every extreme that they name: Each row of edge_rows lists every number 0 to 63 exactly once.
All inputs are finite; a program needn't handle non-finite values.
Results may differ from a plain program's by a relative error of at most 0.00014.
Values sent between devices are 32-bit elements; how exact they have to be, the bound alone decides.
No kernel may reach another device: no remote copies, remote signals or barrier semaphores. Data moves between devices by JAX's collectives and lax.ppermute only.
A program may use at most 64 MiB of HBM per device.

v0:
```python
import jax
import jax.numpy as jnp
from jax import lax
from jax.sharding import PartitionSpec as P

ITERS = 3


def padded(x, sides, width, wrap):
    for axis, dim in sides:
        devices, length = (lax.axis_size(axis), x.shape[dim])
        up = [(i, (i + 1) % devices) for i in range(devices if wrap else devices - 1)]
        down = [(j, i) for i, j in up]
        last = lax.slice_in_dim(x, length - width, length, axis=dim)
        initial = lax.slice_in_dim(x, 0, width, axis=dim)
        before = lax.ppermute(last, axis, up)
        after = lax.ppermute(initial, axis, down)
        x = jnp.concatenate([before, x, after], axis=dim)
    return x


def local_product(left, right):
    return jnp.sum(left * right)


def on_device(right_side, diagonal, horizontal, vertical, precond, edge_rows):
    rows, cols, levels = right_side.shape
    n_gx = lax.axis_size("gx")
    n_gy = lax.axis_size("gy")
    col_index = lax.axis_index("gx")
    row_index = lax.axis_index("gy")
    total_cells = float(rows * cols * levels * n_gx * n_gy)
    half = n_gx // 2
    panel = (col_index >= half).astype(jnp.int32)
    matrix = lax.dynamic_index_in_dim(precond, panel, 0, keepdims=False)
    east_table = jnp.where(col_index == half - 1, edge_rows[0], edge_rows[1])
    west_table = jnp.where(col_index == half, edge_rows[0], edge_rows[1])
    first_row = row_index * rows
    east_local = lax.dynamic_slice_in_dim(east_table, first_row, rows)
    west_local = lax.dynamic_slice_in_dim(west_table, first_row, rows)
    east_border = (col_index == half - 1) | (col_index == n_gx - 1)
    west_border = (col_index == half) | (col_index == 0)
    solution_field = jnp.zeros_like(right_side)
    residual = right_side
    directions = []
    images = []
    norms = []
    for step in range(ITERS):
        pre = jnp.einsum("yxl,kl->yxk", residual, matrix, precision=lax.Precision.HIGHEST)
        wide = padded(pre, (("gx", 1),), 1, True)
        edges = jnp.stack([wide[:, 0], wide[:, -1]], 0)
        whole = lax.all_gather(edges, "gy", axis=1, tiled=True)
        west_fix = jnp.take(whole[0], west_local, axis=0)
        east_fix = jnp.take(whole[1], east_local, axis=0)
        west = jnp.where(west_border, west_fix, edges[0])
        east = jnp.where(east_border, east_fix, edges[1])
        tall = padded(pre, (("gy", 0),), 1, False)
        flat = jnp.pad(pre, ((0, 0), (0, 0), (1, 1)))
        east_side = jnp.concatenate([pre[:, 1:], east[:, None]], 1)
        west_side = jnp.concatenate([west[:, None], pre[:, :-1]], 1)
        beside = east_side + west_side + tall[2:] + tall[:-2]
        column = flat[:, :, 2:] + flat[:, :, :-2]
        image = diagonal * pre + horizontal * (4.0 * pre - beside) + vertical * (2.0 * pre - column)
        count = len(images)
        terms = [local_product(image, older) for older in images]
        terms = terms + [local_product(residual, older) for older in images]
        terms = terms + [local_product(image, image), local_product(residual, image)]
        if step > 0:
            terms.append(local_product(residual, residual))
        totals = lax.psum(jnp.stack(terms), ("gx", "gy")) / total_cells
        coeffs = totals[:count]
        against = totals[count : 2 * count]
        square = totals[2 * count] - jnp.sum(coeffs * coeffs)
        along = totals[2 * count + 1] - jnp.sum(coeffs * against)
        if step > 0:
            norms.append(totals[2 * count + 2])
        for number in range(count):
            pre = pre - coeffs[number] * directions[number]
            image = image - coeffs[number] * images[number]
        scale = 1.0 / jnp.sqrt(square)
        alpha = along * scale
        direction = pre * scale
        image = image * scale
        solution_field = solution_field + alpha * direction
        residual = residual - alpha * image
        directions.append(direction)
        images.append(image)
    norms.append(lax.psum(local_product(residual, residual), ("gx", "gy")) / total_cells)
    return (solution_field, residual, jnp.stack(norms))


def solution(mesh):
    in_specs = (P("gy", "gx", None), P("gy", "gx", None), P("gy", "gx", None), P(), P(), P())
    out_specs = (P("gy", "gx", None), P("gy", "gx", None), P())
    return jax.shard_map(
        on_device, mesh=mesh, in_specs=in_specs, out_specs=out_specs, check_vma=False
    )
```

profile of v0, /device:TPU:0, one launch (start us, length us, event | category | flops | bytes accessed | tf_op | source)
XLA Modules:
  0.0 243.0 jit_solution(2497374235617542815)
XLA Ops:
  0.6 0.0 copy-start
  0.7 0.9 copy-done
  1.5 1.2 convolution_bitcast_fusion
  2.7 1.3 collective-permute-start.2
  4.0 3.0 %collective-permute-start.3 = (f32[1,16,128]{2,1,0:T(8,128)S(1)}, f32[1,16,128]{2,1,0:T(8,128)S(1)}, u32[]{:S(2)}, u32[]{:S(2)}) collective-permute-start(f32[1,16,128]{2,1,0:T(8,128)S(1)} %get-tuple-element.48), channel_id=1, source_target_pairs={{0,1},{1,2},{2,3},{4,5},{5,6},{6,7},{8,9},{9,10},{10,11},{12,13},{... | collective-permute-start | bytes 24584 | tf_op jit(solution)/shard_map/ppermute | solution.py:16
  7.1 3.0 %collective-permute-start = (f32[16,1,128]{2,0,1:T(8,128)S(1)}, f32[16,1,128]{2,0,1:T(8,128)S(1)}, u32[]{:S(2)}, u32[]{:S(2)}) collective-permute-start(f32[16,1,128]{2,0,1:T(8,128)S(1)} %bitcast.112), channel_id=1, source_target_pairs={{0,4},{4,8},{8,12},{12,16},{16,20},{20,24},{24,28},{28,0},{1,5},{5... | collective-permute-start | bytes 24584 | tf_op jit(solution)/shard_map/ppermute | solution.py:16
  10.1 3.1 %collective-permute-start.1 = (f32[16,1,128]{2,0,1:T(8,128)S(1)}, f32[16,1,128]{2,0,1:T(8,128)S(1)}, u32[]{:S(2)}, u32[]{:S(2)}) collective-permute-start(f32[16,1,128]{2,0,1:T(8,128)S(1)} %bitcast.111), channel_id=1, source_target_pairs={{4,0},{8,4},{12,8},{16,12},{20,16},{24,20},{28,24},{0,28},{5,1},{9... | collective-permute-start | bytes 24584 | tf_op jit(solution)/shard_map/ppermute | solution.py:17
  13.3 0.0 copy-start.5
  13.3 0.7 copy-done.5
  14.0 0.1 compare_and_fusion.1
  14.0 0.1 compare_and_fusion
  14.2 0.7 collective-permute-done
  14.8 0.0 collective-permute-done.1
  14.8 5.4 %all_gather.9 = f32[2,64,128]{2,1,0:T(8,128)S(1)} all-gather(f32[2,16,128]{2,1,0:T(8,128)S(1)} %pad_maximum_fusion.6), channel_id=1, replica_groups=mesh['gx'=8,'gy'=4] {'gy'}, dimensions={1}, use_global_device_ids=true | all-gather | bytes 81920 | tf_op jit(solution)/shard_map/all_gather | solution.py:52
  20.2 0.6 gather_fusion
  20.8 0.6 gather_fusion.1
  21.3 0.1 bitcast_select_fusion.5
  21.4 0.1 bitcast_select_fusion.4
  21.5 0.0 collective-permute-done.2
  21.5 0.0 collective-permute-done.3
  21.5 0.0 copy-start.4
  21.5 0.6 copy-done.4
  22.2 0.7 multiply_reduce_fusion.14
  22.9 1.4 pad_maximum_fusion.9
  24.3 40.2 %psum.28 = f32[2]{0:T(128)S(1)} all-reduce(f32[2]{0:T(128)S(1)} %pad_maximum_fusion.9), channel_id=1, replica_groups=mesh['gx'=8,'gy'=4] {'gx','gy'}, use_global_device_ids=true, to_apply=%region_2.4 | all-reduce | flops 2 | bytes 16 | tf_op jit(solution)/shard_map/psum | solution.py:70
  64.5 0.6 fusion.54
  66.5 0.3 fusion.29
  66.8 2.3 collective-permute-start.4
  69.1 2.5 %collective-permute-start.5 = (f32[16,1,128]{2,0,1:T(8,128)S(1)}, f32[16,1,128]{2,0,1:T(8,128)S(1)}, u32[]{:S(2)}, u32[]{:S(2)}) collective-permute-start(f32[16,1,128]{2,0,1:T(8,128)S(1)} %bitcast.113), channel_id=1, source_target_pairs={{4,0},{8,4},{12,8},{16,12},{20,16},{24,20},{28,24},{0,28},{5,1},{9... | collective-permute-start | bytes 24584 | tf_op jit(solution)/shard_map/ppermute | solution.py:17
  71.6 1.3 collective-permute-start.6
  72.9 3.0 %collective-permute-start.7 = (f32[1,16,128]{2,1,0:T(8,128)S(1)}, f32[1,16,128]{2,1,0:T(8,128)S(1)}, u32[]{:S(2)}, u32[]{:S(2)}) collective-permute-start(f32[1,16,128]{2,1,0:T(8,128)S(1)} %get-tuple-element.42), channel_id=1, source_target_pairs={{0,1},{1,2},{2,3},{4,5},{5,6},{6,7},{8,9},{9,10},{10,11},{12,13},{... | collective-permute-start | bytes 24584 | tf_op jit(solution)/shard_map/ppermute | solution.py:16
  75.9 0.0 collective-permute-done.4
  75.9 0.0 collective-permute-done.5
  75.9 5.8 %all_gather.10 = f32[2,64,128]{2,1,0:T(8,128)S(1)} all-gather(f32[2,16,128]{2,1,0:T(8,128)S(1)} %pad_maximum_fusion.7), channel_id=1, replica_groups=mesh['gx'=8,'gy'=4] {'gy'}, dimensions={1}, use_global_device_ids=true | all-gather | bytes 81920 | tf_op jit(solution)/shard_map/all_gather | solution.py:52
  81.8 0.6 gather_fusion.2
  82.3 0.6 gather_fusion.3
  82.9 0.1 bitcast_select_fusion.3
  83.0 0.1 bitcast_select_fusion.2
  83.0 0.0 collective-permute-done.6
  83.0 0.0 collective-permute-done.7
  83.1 0.8 multiply_reduce_fusion.8
  83.8 3.2 %stack.76 = f32[5]{0:T(128)S(1)} concatenate(f32[1]{0:T(128)} %bitcast.28, f32[1]{0:T(128)} %bitcast.29, f32[1]{0:T(128)} %bitcast.30, f32[1]{0:T(128)} %bitcast.31, f32[1]{0:T(128)} %bitcast.32), dimensions={0} | concatenate | bytes 40 | tf_op jit(solution)/shard_map/stack | solution.py:70
  87.1 37.9 %psum.29 = f32[5]{0:T(128)S(1)} all-reduce(f32[5]{0:T(128)S(1)} %stack.76), channel_id=1, replica_groups=mesh['gx'=8,'gy'=4] {'gx','gy'}, use_global_device_ids=true, to_apply=%region_8.10 | all-reduce | flops 5 | bytes 40 | tf_op jit(solution)/shard_map/psum | solution.py:70
  124.9 0.6 fusion.52
  129.4 0.7 multiply_subtract_fusion.1
  130.1 0.3 fusion.27
  130.4 2.3 collective-permute-start.8
  132.7 2.5 %collective-permute-start.9 = (f32[16,1,128]{2,0,1:T(8,128)S(1)}, f32[16,1,128]{2,0,1:T(8,128)S(1)}, u32[]{:S(2)}, u32[]{:S(2)}) collective-permute-start(f32[16,1,128]{2,0,1:T(8,128)S(1)} %bitcast.114), channel_id=1, source_target_pairs={{4,0},{8,4},{12,8},{16,12},{20,16},{24,20},{28,24},{0,28},{5,1},{9... | collective-permute-start | bytes 24584 | tf_op jit(solution)/shard_map/ppermute | solution.py:17
  135.2 1.3 collective-permute-start.10
  136.5 3.0 %collective-permute-start.11 = (f32[1,16,128]{2,1,0:T(8,128)S(1)}, f32[1,16,128]{2,1,0:T(8,128)S(1)}, u32[]{:S(2)}, u32[]{:S(2)}) collective-permute-start(f32[1,16,128]{2,1,0:T(8,128)S(1)} %get-tuple-element.36), channel_id=1, source_target_pairs={{0,1},{1,2},{2,3},{4,5},{5,6},{6,7},{8,9},{9,10},{10,11},{12,13},{... | collective-permute-start | bytes 24584 | tf_op jit(solution)/shard_map/ppermute | solution.py:16
  139.6 5.8 %all_gather.11 = f32[2,64,128]{2,1,0:T(8,128)S(1)} all-gather(f32[2,16,128]{2,1,0:T(8,128)S(1)} %pad_maximum_fusion.8), channel_id=1, replica_groups=mesh['gx'=8,'gy'=4] {'gy'}, dimensions={1}, use_global_device_ids=true | all-gather | bytes 81920 | tf_op jit(solution)/shard_map/all_gather | solution.py:52
  145.4 0.6 gather_fusion.4
  145.9 0.6 gather_fusion.5
  146.5 0.1 bitcast_select_fusion.1
  146.6 0.1 bitcast_select_fusion
  146.7 0.9 multiply_reduce_fusion.1
  147.5 4.5 %stack.85 = f32[7]{0:T(128)S(1)} concatenate(f32[1]{0:T(128)} %bitcast.46, f32[1]{0:T(128)} %bitcast.47, f32[1]{0:T(128)} %bitcast.48, f32[1]{0:T(128)} %bitcast.49, f32[1]{0:T(128)} %bitcast.50, f32[1]{0:T(128)} %bitcast.51, f32[1]{0:T(128)} %bitcast.52), dimensions={0} | concatenate | bytes 56 | tf_op jit(solution)/shard_map/stack | solution.py:70
  152.0 38.1 %psum.30 = f32[7]{0:T(128)S(1)} all-reduce(f32[7]{0:T(128)S(1)} %stack.85), channel_id=1, replica_groups=mesh['gx'=8,'gy'=4] {'gx','gy'}, use_global_device_ids=true, to_apply=%region_16.18 | all-reduce | flops 7 | bytes 56 | tf_op jit(solution)/shard_map/psum | solution.py:70
  190.1 0.8 multiply_reduce_fusion.16
  190.9 0.7 fusion.53
  194.1 2.6 %multiply_add_fusion = f32[16,16,128]{2,1,0:T(8,128)} fusion(f32[16,16,128]{2,1,0:T(8,128)S(1)} %fusion.27, f32[16,16,128]{2,1,0:T(8,128)S(1)} %fusion.29, f32[16,16,128]{2,1,0:T(8,128)S(1)} %convolution_bitcast_fusion, f32[]{:T(128)S(6)} %sqrt.17, f32[]{:T(128)} %bitcast.56, f32[]{:T(128)} %bitcast.55, f32[]{:T(128)S(6)} %mul.267, f32[]{:T(128)} %bitcast.34, ...), kind=kLoop, calls=%fused_computation.51 | loop fusion | flops 458752 | bytes 524324 | tf_op jit(solution)/shard_map/add | solution.py:84
  196.7 2.5 %multiply_reduce_fusion = (f32[]{:T(128)}, f32[16,16,128]{2,1,0:T(8,128)}) fusion(f32[16,16,128]{2,1,0:T(8,128)S(1)} %get-tuple-element.23, f32[]{:T(128)S(6)} %sqrt.17, f32[16,16,128]{2,1,0:T(8,128)S(1)} %get-tuple-element.24, f32[]{:T(128)} %bitcast.56, f32[16,16,128]{2,1,0:T(8,128)S(1)} %get-tuple-element.22, f32[16,16,128]{2,1,0:T(8,128)S(1)} %get-tuple-element.26, ...), kind=kLoop, calls=%fused_computation.49 | loop fusion | flops 327679 | bytes 655384 | tf_op jit(solution)/shard_map/reduce_sum | solution.py:23
  199.2 41.3 %psum.31 = f32[]{:T(128)} all-reduce(f32[]{:T(128)} %get-tuple-element.20), channel_id=1, replica_groups=mesh['gx'=8,'gy'=4] {'gx','gy'}, use_global_device_ids=true, to_apply=%region_20.22 | all-reduce | flops 1 | bytes 8 | tf_op jit(solution)/shard_map/psum | solution.py:88
  241.2 1.8 pad_maximum_fusion.10
  (32 shorter events, 0.2 us)
Async XLA Ops:
  0.6 0.9 copy-start
  2.7 18.8 %collective-permute-start.2 = (f32[1,16,128]{2,1,0:T(8,128)S(1)}, f32[1,16,128]{2,1,0:T(8,128)S(1)}, u32[]{:S(2)}, u32[]{:S(2)}) collective-permute-start(f32[1,16,128]{2,1,0:T(8,128)S(1)} %get-tuple-element.47), channel_id=1, source_target_pairs={{1,0},{2,1},{3,2},{5,4},{6,5},{7,6},{9,8},{10,9},{11,10},{13,12},{... | collective-permute-start | bytes 24584 | tf_op jit(solution)/shard_map/ppermute | solution.py:17
  4.0 17.5 %collective-permute-start.3 = (f32[1,16,128]{2,1,0:T(8,128)S(1)}, f32[1,16,128]{2,1,0:T(8,128)S(1)}, u32[]{:S(2)}, u32[]{:S(2)}) collective-permute-start(f32[1,16,128]{2,1,0:T(8,128)S(1)} %get-tuple-element.48), channel_id=1, source_target_pairs={{0,1},{1,2},{2,3},{4,5},{5,6},{6,7},{8,9},{9,10},{10,11},{12,13},{... | collective-permute-start | bytes 24584 | tf_op jit(solution)/shard_map/ppermute | solution.py:16
  7.1 7.7 %collective-permute-start = (f32[16,1,128]{2,0,1:T(8,128)S(1)}, f32[16,1,128]{2,0,1:T(8,128)S(1)}, u32[]{:S(2)}, u32[]{:S(2)}) collective-permute-start(f32[16,1,128]{2,0,1:T(8,128)S(1)} %bitcast.112), channel_id=1, source_target_pairs={{0,4},{4,8},{8,12},{12,16},{16,20},{20,24},{24,28},{28,0},{1,5},{5... | collective-permute-start | bytes 24584 | tf_op jit(solution)/shard_map/ppermute | solution.py:16
  10.1 4.7 %collective-permute-start.1 = (f32[16,1,128]{2,0,1:T(8,128)S(1)}, f32[16,1,128]{2,0,1:T(8,128)S(1)}, u32[]{:S(2)}, u32[]{:S(2)}) collective-permute-start(f32[16,1,128]{2,0,1:T(8,128)S(1)} %bitcast.111), channel_id=1, source_target_pairs={{4,0},{8,4},{12,8},{16,12},{20,16},{24,20},{28,24},{0,28},{5,1},{9... | collective-permute-start | bytes 24584 | tf_op jit(solution)/shard_map/ppermute | solution.py:17
  13.3 0.7 copy-start.5
  14.8 6.7 %copy-start.3 = (f32[16,16,128]{2,1,0:T(8,128)S(1)}, f32[16,16,128]{2,1,0:T(8,128)}, u32[]{:S(2)}) copy-start(f32[16,16,128]{2,1,0:T(8,128)} %param.9) | copy-start | bytes 393220
  20.2 1.3 copy-start.2
  20.2 1.3 copy-start.1
  21.5 0.7 copy-start.4
  66.8 9.1 %collective-permute-start.4 = (f32[16,1,128]{2,0,1:T(8,128)S(1)}, f32[16,1,128]{2,0,1:T(8,128)S(1)}, u32[]{:S(2)}, u32[]{:S(2)}) collective-permute-start(f32[16,1,128]{2,0,1:T(8,128)S(1)} %bitcast.115), channel_id=1, source_target_pairs={{0,4},{4,8},{8,12},{12,16},{16,20},{20,24},{24,28},{28,0},{1,5},{5... | collective-permute-start | bytes 24584 | tf_op jit(solution)/shard_map/ppermute | solution.py:16
  69.1 6.8 %collective-permute-start.5 = (f32[16,1,128]{2,0,1:T(8,128)S(1)}, f32[16,1,128]{2,0,1:T(8,128)S(1)}, u32[]{:S(2)}, u32[]{:S(2)}) collective-permute-start(f32[16,1,128]{2,0,1:T(8,128)S(1)} %bitcast.113), channel_id=1, source_target_pairs={{4,0},{8,4},{12,8},{16,12},{20,16},{24,20},{28,24},{0,28},{5,1},{9... | collective-permute-start | bytes 24584 | tf_op jit(solution)/shard_map/ppermute | solution.py:17
  71.6 11.5 %collective-permute-start.6 = (f32[1,16,128]{2,1,0:T(8,128)S(1)}, f32[1,16,128]{2,1,0:T(8,128)S(1)}, u32[]{:S(2)}, u32[]{:S(2)}) collective-permute-start(f32[1,16,128]{2,1,0:T(8,128)S(1)} %get-tuple-element.41), channel_id=1, source_target_pairs={{1,0},{2,1},{3,2},{5,4},{6,5},{7,6},{9,8},{10,9},{11,10},{13,12},{... | collective-permute-start | bytes 24584 | tf_op jit(solution)/shard_map/ppermute | solution.py:17
  72.9 10.2 %collective-permute-start.7 = (f32[1,16,128]{2,1,0:T(8,128)S(1)}, f32[1,16,128]{2,1,0:T(8,128)S(1)}, u32[]{:S(2)}, u32[]{:S(2)}) collective-permute-start(f32[1,16,128]{2,1,0:T(8,128)S(1)} %get-tuple-element.42), channel_id=1, source_target_pairs={{0,1},{1,2},{2,3},{4,5},{5,6},{6,7},{8,9},{9,10},{10,11},{12,13},{... | collective-permute-start | bytes 24584 | tf_op jit(solution)/shard_map/ppermute | solution.py:16
  130.4 9.1 %collective-permute-start.8 = (f32[16,1,128]{2,0,1:T(8,128)S(1)}, f32[16,1,128]{2,0,1:T(8,128)S(1)}, u32[]{:S(2)}, u32[]{:S(2)}) collective-permute-start(f32[16,1,128]{2,0,1:T(8,128)S(1)} %bitcast.116), channel_id=1, source_target_pairs={{0,4},{4,8},{8,12},{12,16},{16,20},{20,24},{24,28},{28,0},{1,5},{5... | collective-permute-start | bytes 24584 | tf_op jit(solution)/shard_map/ppermute | solution.py:16
  132.7 6.8 %collective-permute-start.9 = (f32[16,1,128]{2,0,1:T(8,128)S(1)}, f32[16,1,128]{2,0,1:T(8,128)S(1)}, u32[]{:S(2)}, u32[]{:S(2)}) collective-permute-start(f32[16,1,128]{2,0,1:T(8,128)S(1)} %bitcast.114), channel_id=1, source_target_pairs={{4,0},{8,4},{12,8},{16,12},{20,16},{24,20},{28,24},{0,28},{5,1},{9... | collective-permute-start | bytes 24584 | tf_op jit(solution)/shard_map/ppermute | solution.py:17
  135.2 11.5 %collective-permute-start.10 = (f32[1,16,128]{2,1,0:T(8,128)S(1)}, f32[1,16,128]{2,1,0:T(8,128)S(1)}, u32[]{:S(2)}, u32[]{:S(2)}) collective-permute-start(f32[1,16,128]{2,1,0:T(8,128)S(1)} %get-tuple-element.35), channel_id=1, source_target_pairs={{1,0},{2,1},{3,2},{5,4},{6,5},{7,6},{9,8},{10,9},{11,10},{13,12},{... | collective-permute-start | bytes 24584 | tf_op jit(solution)/shard_map/ppermute | solution.py:17
  136.5 10.2 %collective-permute-start.11 = (f32[1,16,128]{2,1,0:T(8,128)S(1)}, f32[1,16,128]{2,1,0:T(8,128)S(1)}, u32[]{:S(2)}, u32[]{:S(2)}) collective-permute-start(f32[1,16,128]{2,1,0:T(8,128)S(1)} %get-tuple-element.36), channel_id=1, source_target_pairs={{0,1},{1,2},{2,3},{4,5},{5,6},{6,7},{8,9},{9,10},{10,11},{12,13},{... | collective-permute-start | bytes 24584 | tf_op jit(solution)/shard_map/ppermute | solution.py:16
where the time goes:
time: 244 us; the launch traced here: 243 us
  blocking collectives  175 us (72%)
  starting transfers between devices  28.6 us (12%)
  local copies, waits for them, and re-layouts  15.2 us (6%)
  other arithmetic  12.7 us (5%)
  between operations  9.45 us (4%)
    psum x3, blocking collectives, on_device(): totals = lax.psum(jnp.stack(terms), ('gx', 'gy')) / total_cells  116 us
    psum x1, blocking collectives, on_device(): lax.psum(local_product(residual, residual), ('gx', 'gy')) / total_cells  41.3 us
    all_gather x3, blocking collectives, on_device(): whole = lax.all_gather(edges, 'gy', axis=1, tiled=True)  17 us
    ppermute x6, starting transfers between devices, padded(): before = lax.ppermute(last, axis, up)  16.8 us
    ppermute x6, starting transfers between devices, padded(): after = lax.ppermute(initial, axis, down)  11.9 us
    another operation x2, local copies, waits for them, and re-layouts, on_device(): totals = lax.psum(jnp.stack(terms), ('gx', 'gy')) / total_cells  7.69 us
    reduce_sum x4, other arithmetic, local_product(): return jnp.sum(left * right)  4.94 us
  transfers between devices with their start and end apart: 12, of which 1 were waited for; matrix products, arithmetic and copies ran while one was open for 2% of the time, Pallas kernels for 0%

commit v1 on v0

v1 whole, which is shorter than its diff:
```python
import functools

import jax
import jax.numpy as jnp
from jax import lax
from jax.experimental import pallas as pl
from jax.experimental.pallas import tpu as pltpu
from jax.sharding import PartitionSpec as P

HI = lax.Precision.HIGHEST
VM = pl.BlockSpec(memory_space=pltpu.VMEM)
SM = pl.BlockSpec(memory_space=pltpu.SMEM)


def krylov_kernel(tbl, meta, r_ref, d_ref, h_ref, before, after, ag, vert_ref, pc_ref,
                  zs_ref, ws_ref, gram_ref, n0_ref, o0_ref, gath_ref, cross_ref, halo_ref):
    rows, cols, lev = r_ref.shape
    n_gy = ag.shape[0]
    high = rows * n_gy
    first = meta[0]
    vert = vert_ref[...]
    m_own = pc_ref[meta[1]]
    m_side = (pc_ref[meta[2]], pc_ref[meta[3]])

    def mul(v, m):
        shape = v.shape
        out = lax.dot_general(v.reshape(-1, lev), m, (((1,), (1,)), ((), ())), precision=HI,
                              preferred_element_type=jnp.float32)
        return out.reshape(shape)

    def column_term(z):
        axis = z.ndim - 1
        lane = lax.broadcasted_iota(jnp.int32, z.shape, axis)
        up = jnp.where(lane == lev - 1, 0.0, pltpu.roll(z, lev - 1, axis))
        down = jnp.where(lane == 0, 0.0, pltpu.roll(z, 1, axis))
        return vert * (2.0 * z - up - down)

    def strip_apply(z, d, h, east, west):
        row = lax.broadcasted_iota(jnp.int32, z.shape, 0)
        north = jnp.where(row == high - 1, 0.0, pltpu.roll(z, high - 1, 0))
        south = jnp.where(row == 0, 0.0, pltpu.roll(z, 1, 0))
        return d * z + h * (4.0 * z - east - west - north - south) + column_term(z)

    def block_apply(z, d, h, halo_e, halo_w):
        mid = z[1:-1]
        col = lax.broadcasted_iota(jnp.int32, mid.shape, 1)
        east = jnp.where(col == cols - 1, halo_e, pltpu.roll(mid, cols - 1, 1))
        west = jnp.where(col == 0, halo_w, pltpu.roll(mid, 1, 1))
        return d * mid + h * (4.0 * mid - east - west - z[2:] - z[:-2]) + column_term(mid)

    def strip(c):
        return jnp.concatenate([ag[g, c] for g in range(n_gy)], 0)

    def gather_rows(side):
        def body(y, _):
            gath_ref[side, pl.ds(y, 1), :] = n0_ref[side, pl.ds(tbl[side, y], 1), :]
            return 0
        lax.fori_loop(0, high, body, 0, unroll=16)

    def gather_own(side):
        def body(y, _):
            cross_ref[side, pl.ds(y, 1), :] = o0_ref[side, pl.ds(tbl[side, y], 1), :]
            return 0
        lax.fori_loop(0, high, body, 0, unroll=16)

    def halo_rows(side, depth):
        for k in range(rows + 2 * depth):
            y = jnp.clip(first - depth + k, 0, high - 1)
            halo_ref[side, k] = n0_ref[side, pl.ds(tbl[side, y], 1), :]
        return halo_ref[side, : rows + 2 * depth]

    r = r_ref[...]
    block = jnp.concatenate([before[0:3], r, after[0:3]], 0)
    d = jnp.concatenate([before[3:5], d_ref[...], after[3:5]], 0)
    h = jnp.concatenate([before[5:7], h_ref[...], after[5:7]], 0)

    own = mul(jnp.stack([strip(c) for c in (0, 1, 4, 5)], 0), m_own)
    o0 = [own[0], own[2]]
    o1 = [own[1], own[3]]
    near = [mul(jnp.stack([strip(8 + 7 * s + c) for c in range(3)], 0), m_side[s]) for s in range(2)]
    for s in range(2):
        n0_ref[s] = near[s][0]
        o0_ref[s] = o0[s]
    z = mul(block, m_own)
    zs_ref[0] = z[3:-3]
    for s in range(2):
        gather_rows(s)
        gather_own(s)
    w_o0 = []
    w_near = []
    for s in range(2):
        base = 8 + 7 * s
        w_o0.append(strip_apply(o0[s], strip(4 * s + 2), strip(4 * s + 3), gath_ref[s], o1[s]))
        a = strip_apply(near[s][0], strip(base + 3), strip(base + 5), near[s][1], cross_ref[s])
        b = strip_apply(near[s][1], strip(base + 4), strip(base + 6), near[s][2], near[s][0])
        w_near.append(jnp.stack([a, b], 0))
    w = block_apply(z, d, h, halo_rows(0, 2), halo_rows(1, 2))
    w0 = w[2:-2]
    ws_ref[0] = w0

    own = mul(jnp.stack(w_o0, 0), m_own)
    near = [mul(w_near[s], m_side[s]) for s in range(2)]
    for s in range(2):
        n0_ref[s] = near[s][0]
        o0_ref[s] = own[s]
    z = mul(w, m_own)
    zs_ref[1] = z[2:-2]
    for s in range(2):
        gather_own(s)
    w_near = []
    for s in range(2):
        base = 8 + 7 * s
        w_near.append(strip_apply(near[s][0], strip(base + 3), strip(base + 5), near[s][1], cross_ref[s]))
    w = block_apply(z, d[1:-1], h[1:-1], halo_rows(0, 1), halo_rows(1, 1))
    w1 = w[1:-1]
    ws_ref[1] = w1

    for s in range(2):
        n0_ref[s] = mul(w_near[s], m_side[s])
    z = mul(w, m_own)
    zs_ref[2] = z[1:-1]
    w2 = block_apply(z, d[2:-2], h[2:-2], halo_rows(0, 0), halo_rows(1, 0))
    ws_ref[2] = w2

    vectors = (r, w0, w1, w2)
    lane = lax.broadcasted_iota(jnp.int32, (1, lev), 1)
    row = jnp.zeros((1, lev), jnp.float32)
    count = 0
    for i in range(4):
        for j in range(i, 4):
            part = jnp.sum(vectors[i] * vectors[j], axis=0)
            part = jnp.sum(jnp.sum(part, axis=0, keepdims=True), axis=1, keepdims=True)
            row = jnp.where(lane == count, part, row)
            count += 1
    gram_ref[...] = jnp.broadcast_to(row[None], gram_ref.shape)


def combine_kernel(parts, r_ref, zs_ref, ws_ref, x_ref, res_ref, norm_ref, *, cells):
    total = jnp.sum(parts[...], axis=0) * (1.0 / cells)
    gram = {}
    count = 0
    for i in range(4):
        for j in range(i, 4):
            gram[i, j] = gram[j, i] = total[:, count : count + 1]
            count += 1

    def inner(a, b):
        out = None
        for i in a:
            for j in b:
                term = a[i] * b[j] * gram[i, j]
                out = term if out is None else out + term
        return out

    def axpy(a, c, b):
        out = dict(a)
        for i in b:
            out[i] = out[i] - c * b[i] if i in out else -c * b[i]
        return out

    one = jnp.ones((1, 1), jnp.float32)
    field = {}
    res = {0: one}
    directions = []
    images = []
    for step in range(3):
        pre = dict(res)
        image = {i + 1: res[i] for i in res}
        coeffs = [inner(image, older) for older in images]
        for c, p, q in zip(coeffs, directions, images):
            pre = axpy(pre, c, p)
            image = axpy(image, c, q)
        scale = 1.0 / jnp.sqrt(inner(image, image))
        pre = {i: pre[i] * scale for i in pre}
        image = {i: image[i] * scale for i in image}
        alpha = inner(res, image)
        field = axpy(field, -alpha, pre)
        res = axpy(res, alpha, image)
        norm_ref[step] = inner(res, res)[0, 0]
        directions.append(pre)
        images.append(image)
    x_ref[...] = field[0] * zs_ref[0] + field[1] * zs_ref[1] + field[2] * zs_ref[2]
    res_ref[...] = res[0] * r_ref[...] + res[1] * ws_ref[0] + res[2] * ws_ref[1] + res[3] * ws_ref[2]


def on_device(right_side, diagonal, horizontal, vertical, precond, edge_rows):
    rows, cols, levels = right_side.shape
    n_gx = lax.axis_size("gx")
    n_gy = lax.axis_size("gy")
    n_dev = n_gx * n_gy
    high = rows * n_gy
    cells = float(rows * cols * levels * n_dev)
    gx = lax.axis_index("gx")
    gy = lax.axis_index("gy")
    half = n_gx // 2
    side_panel = lambda c: (c % n_gx) // half
    own_panel = side_panel(gx)
    east_panel = side_panel(gx + 1)
    west_panel = side_panel(gx + n_gx - 1)
    straight = jnp.arange(high, dtype=jnp.int32)
    east_edge = jnp.where(gx == half - 1, edge_rows[0], edge_rows[1])
    west_edge = jnp.where(gx == half, edge_rows[0], edge_rows[1])
    tbl = jnp.stack([
        jnp.where(east_panel != own_panel, east_edge, straight),
        jnp.where(west_panel != own_panel, west_edge, straight),
    ])
    meta = jnp.stack([gy * rows, own_panel, east_panel, west_panel]).astype(jnp.int32)

    def pack(order):
        arrays = [right_side[:, order[k]] for k in range(3)]
        arrays += [diagonal[:, order[k]] for k in range(2)]
        arrays += [horizontal[:, order[k]] for k in range(2)]
        return jnp.stack(arrays, 0)

    east_pack = pack((cols - 1, cols - 2, cols - 3))
    west_pack = pack((0, 1, 2))
    ring = [(i, (i + 1) % n_gx) for i in range(n_gx)]
    back = [(j, i) for i, j in ring]
    from_east = lax.ppermute(west_pack, "gx", back)
    from_west = lax.ppermute(east_pack, "gx", ring)
    line = [(i, i + 1) for i in range(n_gy - 1)]
    last = jnp.concatenate([right_side[-3:], diagonal[-2:], horizontal[-2:]], 0)
    initial = jnp.concatenate([right_side[:3], diagonal[:2], horizontal[:2]], 0)
    before = lax.ppermute(last, "gy", line)
    after = lax.ppermute(initial, "gy", [(j, i) for i, j in line])
    trim = lambda p: jnp.concatenate([p[0:2], p[3:4], p[5:6]], 0)
    strips = jnp.concatenate([trim(east_pack), trim(west_pack), from_east, from_west], 0)
    ag = lax.all_gather(strips, "gy")

    f32 = jnp.float32
    zs, ws, gram = pl.pallas_call(
        krylov_kernel,
        out_shape=(
            jax.ShapeDtypeStruct((3, rows, cols, levels), f32),
            jax.ShapeDtypeStruct((3, rows, cols, levels), f32),
            jax.ShapeDtypeStruct((n_dev, 1, levels), f32),
        ),
        in_specs=[SM, SM] + [VM] * 8,
        out_specs=(VM, VM, VM),
        scratch_shapes=[pltpu.VMEM((2, high, levels), f32)] * 4
        + [pltpu.VMEM((2, rows + 4, 1, levels), f32)],
        name="krylov",
    )(tbl, meta, right_side, diagonal, horizontal, before, after, ag, vertical[None], precond)

    parts = lax.all_to_all(gram, ("gx", "gy"), 0, 0)
    return pl.pallas_call(
        functools.partial(combine_kernel, cells=cells),
        out_shape=(
            jax.ShapeDtypeStruct((rows, cols, levels), f32),
            jax.ShapeDtypeStruct((rows, cols, levels), f32),
            jax.ShapeDtypeStruct((3,), f32),
        ),
        in_specs=[VM] * 4,
        out_specs=(VM, VM, SM),
        name="combine",
    )(parts, right_side, zs, ws)


def solution(mesh):
    in_specs = (P("gy", "gx", None), P("gy", "gx", None), P("gy", "gx", None), P(), P(), P())
    out_specs = (P("gy", "gx", None), P("gy", "gx", None), P())
    return jax.shard_map(
        on_device, mesh=mesh, in_specs=in_specs, out_specs=out_specs, check_vma=False
    )
```

time: 244 us -> 49.5 us (0.20)
  blocking collectives: 175 us -> 23.8 us
  starting transfers between devices: 28.6 us -> 9.22 us
  other arithmetic: 12.7 us -> 1.16 us
  between operations: 9.45 us -> 0.77 us
  local copies, waits for them, and re-layouts: 15.2 us -> 6.57 us
  Pallas kernels: 0 us -> 7.16 us
    psum x4 -> x0, blocking collectives: 158 us -> none  [the longest x3 116 us: on_device(): totals = lax.psum(jnp.stack(terms), ('gx', 'gy')) / total_cells]
    ppermute x12 -> x4, starting transfers between devices: 28.6 us -> 9.22 us  [the longest x1 3.14 us: on_device(): from_east = lax.ppermute(west_pack, 'gx', back)]
    all_to_all x0 -> x1, blocking collectives: none -> 12.5 us  [on_device(): parts = lax.all_to_all(gram, ('gx', 'gy'), 0, 0)]
    another operation x2, local copies, waits for them, and re-layouts: 7.69 us -> 0.01 us  [pack(): return jnp.stack(arrays, 0)]
    pallas_call x0 -> x2, Pallas kernels: none -> 7.16 us  [the longest x1 4.91 us: on_device(): pl.pallas_call(krylov_kernel, out_shape=(jax.ShapeDtypeStruct((3, rows, c...]
    reduce_sum x5 -> x0, other arithmetic: 5.7 us -> none  [the longest x4 4.94 us: local_product(): return jnp.sum(left * right)]
    all_gather x3 -> x1, blocking collectives: 17 us -> 11.3 us  [on_device(): ag = lax.all_gather(strips, 'gy')]
    gather x6 -> x0, local copies, waits for them, and re-layouts: 3.37 us -> none  [the longest x3 1.69 us: on_device(): west_fix = jnp.take(whole[0], west_local, axis=0)]
  transfers between devices with their start and end apart: 12 -> 4, of which waited for: 1 -> 1; matrix products, arithmetic and copies ran while one was open for 2% -> 9% of each run, Pallas kernels for 0% -> 0%
where the time goes in v1:
time: 49.5 us; the launch traced here: 48.9 us
  blocking collectives  23.8 us (48%)
  starting transfers between devices  9.22 us (19%)
  Pallas kernels  7.16 us (14%)
  local copies, waits for them, and re-layouts  6.57 us (13%)
  other arithmetic  1.16 us (2%)
  between operations  0.77 us (2%)
    all_to_all x1, blocking collectives, on_device(): parts = lax.all_to_all(gram, ('gx', 'gy'), 0, 0)  12.5 us
    all_gather x1, blocking collectives, on_device(): ag = lax.all_gather(strips, 'gy')  11.3 us
    pallas_call x1, Pallas kernels, on_device(): pl.pallas_call(krylov_kernel, out_shape=(jax.ShapeDtypeStruct((3, rows, c...  4.91 us
    ppermute x1, starting transfers between devices, on_device(): from_east = lax.ppermute(west_pack, 'gx', back)  3.14 us
    ppermute x1, starting transfers between devices, on_device(): before = lax.ppermute(last, 'gy', line)  2.4 us
    ppermute x1, starting transfers between devices, on_device(): from_west = lax.ppermute(east_pack, 'gx', ring)  2.39 us
    pallas_call x1, Pallas kernels, on_device(): pl.pallas_call(functools.partial(combine_kernel, cells=cells), out_shape=...  2.25 us
    slice x3, local copies, waits for them, and re-layouts, on_device(): initial = jnp.concatenate([right_side[:3], diagonal[:2], horizontal[:2]], 0)  2.24 us
  transfers between devices with their start and end apart: 4, of which 1 were waited for; matrix products, arithmetic and copies ran while one was open for 9% of the time, Pallas kernels for 0%

profile of v1, /device:TPU:0, one launch (start us, length us, event | category | flops | bytes accessed | tf_op | source)
XLA Modules:
  0.0 48.9 jit_solution(5513056356102866076)
XLA Ops:
  0.6 0.7 %fusion.4 = (f32[2,16,128]{2,1,0:T(8,128)S(1)}, f32[2,16,128]{2,1,0:T(8,128)S(1)}) fusion(f32[16,16,128]{2,1,0:T(8,128)} %d_ref.1), kind=kLoop, calls=%fused_computation.36 | loop fusion | bytes 65536 | tf_op jit(solution)/shard_map/slice | solution.py:223
  1.4 0.7 %fusion.5 = (f32[2,16,128]{2,1,0:T(8,128)S(1)}, f32[2,16,128]{2,1,0:T(8,128)S(1)}) fusion(f32[16,16,128]{2,1,0:T(8,128)} %h_ref.1), kind=kLoop, calls=%fused_computation.37 | loop fusion | bytes 65536 | tf_op jit(solution)/shard_map/slice | solution.py:223
  2.1 0.8 %fusion.3 = (f32[3,16,128]{2,1,0:T(8,128)S(1)}, f32[3,16,128]{2,1,0:T(8,128)S(1)}) fusion(f32[16,16,128]{2,1,0:T(8,128)} %r_ref.3), kind=kLoop, calls=%fused_computation.35 | loop fusion | bytes 98304 | tf_op jit(solution)/shard_map/slice | solution.py:223
  2.9 2.4 %collective-permute-start = (f32[7,16,128]{2,1,0:T(8,128)S(1)}, f32[7,16,128]{2,1,0:T(8,128)S(1)}, u32[]{:S(2)}, u32[]{:S(2)}) collective-permute-start(f32[7,16,128]{2,1,0:T(8,128)S(1)} %pad_maximum_fusion), channel_id=1, source_target_pairs={{0,1},{1,2},{2,3},{4,5},{5,6},{6,7},{8,9},{9,10},{10,11},{12,13},{... | collective-permute-start | bytes 172040 | tf_op jit(solution)/shard_map/ppermute | solution.py:224
  5.3 1.3 %collective-permute-start.1 = (f32[7,16,128]{2,1,0:T(8,128)S(1)}, f32[7,16,128]{2,1,0:T(8,128)S(1)}, u32[]{:S(2)}, u32[]{:S(2)}) collective-permute-start(f32[7,16,128]{2,1,0:T(8,128)S(1)} %pad_maximum_fusion.1), channel_id=1, source_target_pairs={{1,0},{2,1},{3,2},{5,4},{6,5},{7,6},{9,8},{10,9},{11,10},{13,12},{... | collective-permute-start | bytes 172040 | tf_op jit(solution)/shard_map/ppermute | solution.py:225
  6.6 1.0 %fusion.1 = (f32[16,1,128]{2,1,0:T(1,128)S(1)}, f32[16,1,128]{2,1,0:T(1,128)S(1)}, f32[16,1,128]{2,1,0:T(1,128)S(1)}, f32[16,1,128]{2,1,0:T(1,128)S(1)}) fusion(f32[16,16,128]{2,1,0:T(8,128)} %d_ref.1), kind=kLoop, calls=%fused_computation.33 | loop fusion | bytes 65536 | tf_op jit(solution)/shard_map/slice | solution.py:211
  7.6 1.0 %fusion = (f32[16,1,128]{2,1,0:T(1,128)S(1)}, f32[16,1,128]{2,1,0:T(1,128)S(1)}, f32[16,1,128]{2,1,0:T(1,128)S(1)}, f32[16,1,128]{2,1,0:T(1,128)S(1)}) fusion(f32[16,16,128]{2,1,0:T(8,128)} %h_ref.1), kind=kLoop, calls=%fused_computation.32 | loop fusion | bytes 65536 | tf_op jit(solution)/shard_map/slice | solution.py:212
  8.5 1.0 %fusion.2 = (f32[16,1,128]{2,1,0:T(1,128)S(1)}, f32[16,1,128]{2,1,0:T(1,128)S(1)}, f32[16,1,128]{2,1,0:T(1,128)S(1)}, f32[16,1,128]{2,1,0:T(1,128)S(1)}, f32[16,...) fusion(f32[16,16,128]{2,1,0:T(8,128)} %r_ref.3), kind=kLoop, calls=%fused_computation.34 | loop fusion | bytes 98304 | tf_op jit(solution)/shard_map/slice | solution.py:210
  9.7 2.4 %collective-permute-start.3 = (f32[7,16,128]{2,1,0:T(8,128)S(1)}, f32[7,16,128]{2,1,0:T(8,128)S(1)}, u32[]{:S(2)}, u32[]{:S(2)}) collective-permute-start(f32[7,16,128]{2,1,0:T(8,128)S(1)} %constant_dynamic-update-slice_fusion.7), channel_id=1, source_target_pairs={{0,4},{4,8},{8,12},{12,16},{16,20},{20,24},{24,28},{28,0},{1,5},{5... | collective-permute-start | bytes 172040 | tf_op jit(solution)/shard_map/ppermute | solution.py:220
  12.1 3.1 %collective-permute-start.2 = (f32[7,16,128]{2,1,0:T(8,128)S(1)}, f32[7,16,128]{2,1,0:T(8,128)S(1)}, u32[]{:S(2)}, u32[]{:S(2)}) collective-permute-start(f32[7,16,128]{2,1,0:T(8,128)S(1)} %constant_dynamic-update-slice_fusion), channel_id=1, source_target_pairs={{4,0},{8,4},{12,8},{16,12},{20,16},{24,20},{28,24},{0,28},{5,1},{9... | collective-permute-start | bytes 172040 | tf_op jit(solution)/shard_map/ppermute | solution.py:219
  15.2 0.0 copy-start.2
  15.2 0.7 %copy-done.2 = s32[2,64]{1,0:T(2,128)S(1)} copy-done((s32[2,64]{1,0:T(2,128)S(1)}, s32[2,64]{1,0:T(2,128)}, u32[]{:S(2)}) %copy-start.2) | copy-done | bytes 536
  15.9 0.6 %pad_add_fusion.tbl = s32[2,64]{1,0:T(2,128)} fusion(s32[1,64]{1,0:T(1,128)S(1)} %get-tuple-element.46, s32[1,64]{1,0:T(1,128)S(1)} %get-tuple-element.45), kind=kLoop, calls=%fused_computation.26 | loop fusion | flops 128 | bytes 1024 | tf_op jit(solution)/shard_map/stack | solution.py:203
  16.5 0.6 %pad_add_fusion.1.meta = s32[4]{0:T(128)} fusion(s32[1]{0:T(128)} %bitcast.3, s32[1]{0:T(128)} %bitcast.2, s32[1]{0:T(128)} %bitcast.1, s32[1]{0:T(128)} %bitcast), kind=kLoop, calls=%fused_computation.31 | loop fusion | flops 12 | bytes 32 | tf_op jit(solution)/shard_map/stack | solution.py:207
  17.1 0.0 collective-permute-done.2
  17.1 0.2 collective-permute-done.3
  17.3 11.3 %all-gather = f32[88,16,128]{2,1,0:T(8,128)} all-gather(f32[22,16,128]{2,1,0:T(8,128)S(1)} %constant_dynamic-update-slice_fusion.14), channel_id=2, replica_groups=mesh['gx'=8,'gy'=4] {'gy'}, dimensions={0}, use_global_device_ids=true | all-gather | bytes 901120 | tf_op jit(solution)/shard_map/all_gather | solution.py:228
  28.6 0.0 collective-permute-done.before
  28.6 0.0 copy-start
  28.6 0.0 collective-permute-done.1.after
  28.6 0.0 copy-start.1
  28.6 0.6 %copy-done = f32[7,16,128]{2,1,0:T(8,128)} copy-done((f32[7,16,128]{2,1,0:T(8,128)}, f32[7,16,128]{2,1,0:T(8,128)S(1)}, u32[]{:S(2)}) %copy-start) | copy-done | bytes 57368
  29.2 0.0 copy-done.1
  29.3 4.9 %krylov.1 = (f32[3,16,16,128]{3,2,1,0:T(8,128)}, f32[3,16,16,128]{3,2,1,0:T(8,128)}, f32[32,1,128]{2,1,0:T(1,128)}) custom-call(s32[2,64]{1,0:T(2,128)} %pad_add_fusion.tbl, s32[4]{0:T(128)} %pad_add_fusion.1.meta, f32[16,16,128]{2,1,0:T(8,128)} %r_ref.3, f32[16,16,128]{2,1,0:T(8,128)} %d_ref.1, f32[16,16,128]{2,1,0:T(8,128)} %h_ref.1, ...), custom_call_target="tpu_custom_call" | custom-call | tf_op jit(solution)/shard_map/krylov/pallas_call | solution.py:231
  34.2 12.5 %all_to_all.5.parts = f32[32,1,128]{2,1,0:T(1,128)} all-to-all(f32[32,1,128]{2,1,0:T(1,128)} %get-tuple-element.6), channel_id=1, replica_groups=mesh['gx'=8,'gy'=4] {'gx','gy'}, dimensions={0} | all-to-all | bytes 32768 | tf_op jit(solution)/shard_map/all_to_all | solution.py:245
  46.7 2.2 %combine.1 = (f32[16,16,128]{2,1,0:T(8,128)}, f32[16,16,128]{2,1,0:T(8,128)}, f32[3]{0:T(128)}) custom-call(f32[32,1,128]{2,1,0:T(1,128)} %all_to_all.5.parts, f32[16,16,128]{2,1,0:T(8,128)} %r_ref.3, f32[3,16,16,128]{3,2,1,0:T(8,128)} %get-tuple-element.7.zs_ref, f32[3,16,16,128]{3,2,1,0:T(8,128)} %get-tuple-element.8.ws_ref), custom_call_target="tpu_custom_call" | custom-call | tf_op jit(solution)/shard_map/combine/pallas_call | solution.py:246
  (19 shorter events, 0.1 us)
Async XLA Ops:
  2.9 25.7 %collective-permute-start = (f32[7,16,128]{2,1,0:T(8,128)S(1)}, f32[7,16,128]{2,1,0:T(8,128)S(1)}, u32[]{:S(2)}, u32[]{:S(2)}) collective-permute-start(f32[7,16,128]{2,1,0:T(8,128)S(1)} %pad_maximum_fusion), channel_id=1, source_target_pairs={{0,1},{1,2},{2,3},{4,5},{5,6},{6,7},{8,9},{9,10},{10,11},{12,13},{... | collective-permute-start | bytes 172040 | tf_op jit(solution)/shard_map/ppermute | solution.py:224
  5.3 23.3 %collective-permute-start.1 = (f32[7,16,128]{2,1,0:T(8,128)S(1)}, f32[7,16,128]{2,1,0:T(8,128)S(1)}, u32[]{:S(2)}, u32[]{:S(2)}) collective-permute-start(f32[7,16,128]{2,1,0:T(8,128)S(1)} %pad_maximum_fusion.1), channel_id=1, source_target_pairs={{1,0},{2,1},{3,2},{5,4},{6,5},{7,6},{9,8},{10,9},{11,10},{13,12},{... | collective-permute-start | bytes 172040 | tf_op jit(solution)/shard_map/ppermute | solution.py:225
  9.7 7.6 %collective-permute-start.3 = (f32[7,16,128]{2,1,0:T(8,128)S(1)}, f32[7,16,128]{2,1,0:T(8,128)S(1)}, u32[]{:S(2)}, u32[]{:S(2)}) collective-permute-start(f32[7,16,128]{2,1,0:T(8,128)S(1)} %constant_dynamic-update-slice_fusion.7), channel_id=1, source_target_pairs={{0,4},{4,8},{8,12},{12,16},{16,20},{20,24},{24,28},{28,0},{1,5},{5... | collective-permute-start | bytes 172040 | tf_op jit(solution)/shard_map/ppermute | solution.py:220
  12.1 5.0 %collective-permute-start.2 = (f32[7,16,128]{2,1,0:T(8,128)S(1)}, f32[7,16,128]{2,1,0:T(8,128)S(1)}, u32[]{:S(2)}, u32[]{:S(2)}) collective-permute-start(f32[7,16,128]{2,1,0:T(8,128)S(1)} %constant_dynamic-update-slice_fusion), channel_id=1, source_target_pairs={{4,0},{8,4},{12,8},{16,12},{20,16},{24,20},{28,24},{0,28},{5,1},{9... | collective-permute-start | bytes 172040 | tf_op jit(solution)/shard_map/ppermute | solution.py:219
  15.2 0.7 %copy-start.2 = (s32[2,64]{1,0:T(2,128)S(1)}, s32[2,64]{1,0:T(2,128)}, u32[]{:S(2)}) copy-start(s32[2,64]{1,0:T(2,128)} %param.11) | copy-start | bytes 1540
  28.6 0.6 %copy-start = (f32[7,16,128]{2,1,0:T(8,128)}, f32[7,16,128]{2,1,0:T(8,128)S(1)}, u32[]{:S(2)}) copy-start(f32[7,16,128]{2,1,0:T(8,128)S(1)} %collective-permute-done.before) | copy-start | bytes 172036
  28.6 0.6 %copy-start.1 = (f32[7,16,128]{2,1,0:T(8,128)}, f32[7,16,128]{2,1,0:T(8,128)S(1)}, u32[]{:S(2)}) copy-start(f32[7,16,128]{2,1,0:T(8,128)S(1)} %collective-permute-done.1.after) | copy-start | bytes 172036

commit v2 on v1

v2 whole, which is shorter than its diff:
```python
import functools

import jax
import jax.numpy as jnp
from jax import lax
from jax.experimental import pallas as pl
from jax.experimental.pallas import tpu as pltpu
from jax.sharding import PartitionSpec as P

PAD = 8
HI = lax.Precision.HIGHEST
VM = pl.BlockSpec(memory_space=pltpu.VMEM)
SM = pl.BlockSpec(memory_space=pltpu.SMEM)


def position(n_gx):
    gx = lax.axis_index("gx")
    half = n_gx // 2
    east = (gx == half - 1) | (gx == n_gx - 1)
    west = (gx == half) | (gx == 0)
    return gx, half, east, west


def pack_kernel(r_ref, d_ref, h_ref, east_ref, west_ref):
    cols = r_ref.shape[1]
    slot = 0
    for ref, depth in ((r_ref, 3), (d_ref, 2), (h_ref, 2)):
        for k in range(depth):
            east_ref[slot] = ref[:, cols - 1 - k, :]
            west_ref[slot] = ref[:, k, :]
            slot += 1


def widen_kernel(r_ref, d_ref, h_ref, east_own, west_own, east_ref, west_ref,
                 rw_ref, dw_ref, hw_ref, last_ref, first_ref, strip_ref, *, n_gx):
    rows, cols, lev = r_ref.shape
    _, _, seam_east, _ = position(n_gx)
    slot = 0
    for ref, wide, depth in ((r_ref, rw_ref, 3), (d_ref, dw_ref, 2), (h_ref, hw_ref, 2)):
        wide[:, :cols, :] = ref[...]
        wide[:, cols:, :] = jnp.zeros((rows, PAD, lev), jnp.float32)
        for k in range(depth):
            wide[:, cols + k, :] = east_ref[slot + k]
            wide[:, cols + PAD - 1 - k, :] = west_ref[slot + k]
        last_ref[slot : slot + depth] = wide[rows - depth :]
        first_ref[slot : slot + depth] = wide[:depth]
        slot += depth
    for place, k in enumerate((0, 1, 3, 5)):
        strip_ref[place] = jnp.where(seam_east, east_own[k], west_own[k])
    for k in range(7):
        strip_ref[4 + k] = jnp.where(seam_east, east_ref[k], west_ref[k])


def krylov_kernel(edges, rw_ref, dw_ref, hw_ref, before, after, ag, vert_ref, pc_ref,
                  zs_ref, ws_ref, gram_ref, n0_ref, o0_ref, gath_ref, cross_ref, halo_ref, *, n_gx):
    rows, wide, lev = rw_ref.shape
    cols = wide - PAD
    n_gy = ag.shape[0]
    high = rows * n_gy
    first = lax.axis_index("gy") * rows
    gx, half, seam_east, seam_west = position(n_gx)
    table = jnp.where((gx == half - 1) | (gx == half), 0, 1)
    seam_col = jnp.where(seam_east, cols, jnp.where(seam_west, wide - 1, -1))
    panel = gx // half
    vert = vert_ref[...]
    m_own = pc_ref[panel]
    m_near = pc_ref[1 - panel]

    def mul(v, m):
        shape = v.shape
        out = lax.dot_general(v.reshape(-1, lev), m, (((1,), (1,)), ((), ())), precision=HI,
                              preferred_element_type=jnp.float32)
        return out.reshape(shape)

    def column_term(z):
        axis = z.ndim - 1
        lane = lax.broadcasted_iota(jnp.int32, z.shape, axis)
        up = jnp.where(lane == lev - 1, 0.0, pltpu.roll(z, lev - 1, axis))
        down = jnp.where(lane == 0, 0.0, pltpu.roll(z, 1, axis))
        return vert * (2.0 * z - up - down)

    def strip_apply(z, d, h, east, west):
        row = lax.broadcasted_iota(jnp.int32, z.shape, 0)
        north = jnp.where(row == high - 1, 0.0, pltpu.roll(z, high - 1, 0))
        south = jnp.where(row == 0, 0.0, pltpu.roll(z, 1, 0))
        return d * z + h * (4.0 * z - east - west - north - south) + column_term(z)

    def block_apply(z, d, h, depth):
        for k in range(rows + 2 * depth):
            y = jnp.clip(first - depth + k, 0, high - 1)
            halo_ref[k] = n0_ref[pl.ds(edges[table, y], 1), :]
        mid = z[1:-1]
        col = lax.broadcasted_iota(jnp.int32, mid.shape, 1)
        mid = jnp.where(col == seam_col, halo_ref[: rows + 2 * depth], mid)
        beside = pltpu.roll(mid, wide - 1, 1) + pltpu.roll(mid, 1, 1) + z[2:] + z[:-2]
        return d * mid + h * (4.0 * mid - beside) + column_term(mid)

    def strip(c):
        return jnp.concatenate([ag[g, c] for g in range(n_gy)], 0)

    def gather(source, target):
        def body(y, _):
            target[pl.ds(y, 1), :] = source[pl.ds(edges[table, y], 1), :]
            return 0
        lax.fori_loop(0, high, body, 0, unroll=16)

    block = jnp.concatenate([before[0:3], rw_ref[...], after[0:3]], 0)
    d = jnp.concatenate([before[3:5], dw_ref[...], after[3:5]], 0)
    h = jnp.concatenate([before[5:7], hw_ref[...], after[5:7]], 0)

    own = mul(jnp.stack([strip(0), strip(1)], 0), m_own)
    near = mul(jnp.stack([strip(4), strip(5), strip(6)], 0), m_near)
    n0_ref[...] = near[0]
    o0_ref[...] = own[0]
    gather(n0_ref, gath_ref)
    gather(o0_ref, cross_ref)
    z = mul(block, m_own)
    zs_ref[0] = z[3:-3, :cols]
    w_o0 = strip_apply(own[0], strip(2), strip(3), gath_ref[...], own[1])
    w_n0 = strip_apply(near[0], strip(7), strip(9), near[1], cross_ref[...])
    w_n1 = strip_apply(near[1], strip(8), strip(10), near[2], near[0])
    w = block_apply(z, d, h, 2)
    w0 = w[2:-2, :cols]
    ws_ref[0] = w0

    o0_ref[...] = mul(w_o0, m_own)
    near = mul(jnp.stack([w_n0, w_n1], 0), m_near)
    n0_ref[...] = near[0]
    gather(o0_ref, cross_ref)
    z = mul(w, m_own)
    zs_ref[1] = z[2:-2, :cols]
    w_n0 = strip_apply(near[0], strip(7), strip(9), near[1], cross_ref[...])
    w = block_apply(z, d[1:-1], h[1:-1], 1)
    w1 = w[1:-1, :cols]
    ws_ref[1] = w1

    n0_ref[...] = mul(w_n0, m_near)
    z = mul(w, m_own)
    zs_ref[2] = z[1:-1, :cols]
    w2 = block_apply(z, d[2:-2], h[2:-2], 0)[:, :cols]
    ws_ref[2] = w2

    vectors = (rw_ref[:, :cols, :], w0, w1, w2)
    lane = lax.broadcasted_iota(jnp.int32, (1, lev), 1)
    row = jnp.zeros((1, lev), jnp.float32)
    count = 0
    for i in range(4):
        for j in range(i, 4):
            part = jnp.sum(vectors[i] * vectors[j], axis=0)
            part = jnp.sum(jnp.sum(part, axis=0, keepdims=True), axis=1, keepdims=True)
            row = jnp.where(lane == count, part, row)
            count += 1
    gram_ref[...] = jnp.broadcast_to(row[None], gram_ref.shape)


def combine_kernel(parts, r_ref, zs_ref, ws_ref, x_ref, res_ref, norm_ref, *, cells):
    total = jnp.sum(parts[...], axis=0) * (1.0 / cells)
    gram = {}
    count = 0
    for i in range(4):
        for j in range(i, 4):
            gram[i, j] = gram[j, i] = total[:, count : count + 1]
            count += 1

    def inner(a, b):
        out = None
        for i in a:
            for j in b:
                term = a[i] * b[j] * gram[i, j]
                out = term if out is None else out + term
        return out

    def axpy(a, c, b):
        out = dict(a)
        for i in b:
            out[i] = out[i] - c * b[i] if i in out else -c * b[i]
        return out

    one = jnp.ones((1, 1), jnp.float32)
    field = {}
    res = {0: one}
    directions = []
    images = []
    for step in range(3):
        pre = dict(res)
        image = {i + 1: res[i] for i in res}
        coeffs = [inner(image, older) for older in images]
        for c, p, q in zip(coeffs, directions, images):
            pre = axpy(pre, c, p)
            image = axpy(image, c, q)
        scale = 1.0 / jnp.sqrt(inner(image, image))
        pre = {i: pre[i] * scale for i in pre}
        image = {i: image[i] * scale for i in image}
        alpha = inner(res, image)
        field = axpy(field, -alpha, pre)
        res = axpy(res, alpha, image)
        norm_ref[step] = inner(res, res)[0, 0]
        directions.append(pre)
        images.append(image)
    x_ref[...] = field[0] * zs_ref[0] + field[1] * zs_ref[1] + field[2] * zs_ref[2]
    res_ref[...] = res[0] * r_ref[...] + res[1] * ws_ref[0] + res[2] * ws_ref[1] + res[3] * ws_ref[2]


def on_device(right_side, diagonal, horizontal, vertical, precond, edge_rows):
    rows, cols, levels = right_side.shape
    n_gx = lax.axis_size("gx")
    n_gy = lax.axis_size("gy")
    n_dev = n_gx * n_gy
    assert n_gx >= 4 and cols >= 3 and cols % 8 == 0
    high = rows * n_gy
    wide = cols + PAD
    cells = float(rows * cols * levels * n_dev)
    f32 = jnp.float32
    shaped = lambda *shape: jax.ShapeDtypeStruct(shape, f32)

    east_pack, west_pack = pl.pallas_call(
        pack_kernel,
        out_shape=(shaped(7, rows, levels),) * 2,
        in_specs=[VM] * 3,
        out_specs=(VM,) * 2,
        name="pack",
    )(right_side, diagonal, horizontal)
    ring = [(i, (i + 1) % n_gx) for i in range(n_gx)]
    from_west = lax.ppermute(east_pack, "gx", ring)
    from_east = lax.ppermute(west_pack, "gx", [(j, i) for i, j in ring])
    rw, dw, hw, last, initial, strips = pl.pallas_call(
        functools.partial(widen_kernel, n_gx=n_gx),
        out_shape=(shaped(rows, wide, levels),) * 3 + (shaped(7, wide, levels),) * 2 + (shaped(11, rows, levels),),
        in_specs=[VM] * 7,
        out_specs=(VM,) * 6,
        name="widen",
    )(right_side, diagonal, horizontal, east_pack, west_pack, from_east, from_west)
    line = [(i, i + 1) for i in range(n_gy - 1)]
    before = lax.ppermute(last, "gy", line)
    after = lax.ppermute(initial, "gy", [(j, i) for i, j in line])
    ag = lax.all_gather(strips, "gy")

    zs, ws, gram = pl.pallas_call(
        functools.partial(krylov_kernel, n_gx=n_gx),
        out_shape=(shaped(3, rows, cols, levels), shaped(3, rows, cols, levels), shaped(n_dev, 1, levels)),
        in_specs=[SM] + [VM] * 8,
        out_specs=(VM, VM, VM),
        scratch_shapes=[pltpu.VMEM((high, levels), f32)] * 4
        + [pltpu.VMEM((rows + 4, 1, levels), f32)],
        name="krylov",
    )(edge_rows, rw, dw, hw, before, after, ag, vertical[None], precond)

    parts = lax.all_to_all(gram, ("gx", "gy"), 0, 0)
    return pl.pallas_call(
        functools.partial(combine_kernel, cells=cells),
        out_shape=(
            jax.ShapeDtypeStruct((rows, cols, levels), f32),
            jax.ShapeDtypeStruct((rows, cols, levels), f32),
            jax.ShapeDtypeStruct((3,), f32),
        ),
        in_specs=[VM] * 4,
        out_specs=(VM, VM, SM),
        name="combine",
    )(parts, right_side, zs, ws)


def solution(mesh):
    in_specs = (P("gy", "gx", None), P("gy", "gx", None), P("gy", "gx", None), P(), P(), P())
    out_specs = (P("gy", "gx", None), P("gy", "gx", None), P())
    return jax.shard_map(
        on_device, mesh=mesh, in_specs=in_specs, out_specs=out_specs, check_vma=False
    )
```

time: 49.5 us -> 47.4 us (0.958)
  local copies, waits for them, and re-layouts: 6.57 us -> 1.68 us
  Pallas kernels: 7.16 us -> 10.8 us
  waiting for transfers between devices: 0.22 us -> 2.58 us
  other arithmetic: 1.16 us -> 0 us
  blocking collectives: 23.8 us -> 22.7 us
  starting transfers between devices: 9.22 us -> 8.61 us
    slice x6 -> x0, local copies, waits for them, and re-layouts: 5.21 us -> none  [the longest x3 2.24 us: on_device(): initial = jnp.concatenate([right_side[:3], diagonal[:2], horizontal[:2]], 0)]
    pallas_call x1 -> x3, Pallas kernels: 4.91 us -> 8.59 us  [the longest x1 4.8 us: on_device(): pl.pallas_call(functools.partial(krylov_kernel, n_gx=n_gx), out_shape=(sh...]
    ppermute x1, waiting for transfers between devices: 0.21 us -> 2.36 us  [on_device(): from_west = lax.ppermute(east_pack, 'gx', ring)]
    another operation x2 -> x0, other arithmetic: 1.14 us -> none  [the longest x1 0.59 us: on_device(): jnp.stack([jnp.where(east_panel != own_panel, east_edge, straight), jnp.w...]
    ppermute x1, starting transfers between devices: 2.4 us -> 1.28 us  [on_device(): before = lax.ppermute(last, 'gy', line)]
    all_to_all x1, blocking collectives: 12.5 us -> 11.9 us  [on_device(): parts = lax.all_to_all(gram, ('gx', 'gy'), 0, 0)]
    ppermute x1, starting transfers between devices: 2.39 us -> 3 us  [on_device(): from_west = lax.ppermute(east_pack, 'gx', ring)]
    all_gather x1, blocking collectives: 11.3 us -> 10.8 us  [on_device(): ag = lax.all_gather(strips, 'gy')]
  transfers between devices with their start and end apart: 4 -> 4, of which waited for: 1 -> 2; matrix products, arithmetic and copies ran while one was open for 9% -> 0% of each run, Pallas kernels for 0% -> 0%
where the time goes in v2:
time: 47.4 us; the launch traced here: 47 us
  blocking collectives  22.7 us (48%)
  Pallas kernels  10.8 us (23%)
  starting transfers between devices  8.61 us (18%)
  waiting for transfers between devices  2.58 us (5%)
  local copies, waits for them, and re-layouts  1.68 us (4%)
  between operations  0.66 us (1%)
    all_to_all x1, blocking collectives, on_device(): parts = lax.all_to_all(gram, ('gx', 'gy'), 0, 0)  11.9 us
    all_gather x1, blocking collectives, on_device(): ag = lax.all_gather(strips, 'gy')  10.8 us
    pallas_call x1, Pallas kernels, on_device(): pl.pallas_call(functools.partial(krylov_kernel, n_gx=n_gx), out_shape=(sh...  4.8 us
    ppermute x1, starting transfers between devices, on_device(): from_east = lax.ppermute(west_pack, 'gx', [(j, i) for i, j in ring])  3.04 us
    ppermute x1, starting transfers between devices, on_device(): from_west = lax.ppermute(east_pack, 'gx', ring)  3 us
    ppermute x1, waiting for transfers between devices, on_device(): from_west = lax.ppermute(east_pack, 'gx', ring)  2.36 us
    pallas_call x1, Pallas kernels, on_device(): pl.pallas_call(functools.partial(combine_kernel, cells=cells), out_shape=...  2.25 us
    pallas_call x1, Pallas kernels, on_device(): pl.pallas_call(functools.partial(widen_kernel, n_gx=n_gx), out_shape=(sha...  2.04 us
  transfers between devices with their start and end apart: 4, of which 2 were waited for; matrix products, arithmetic and copies ran while one was open for 0% of the time, Pallas kernels for 0%

profile of v2, /device:TPU:0, one launch (start us, length us, event | category | flops | bytes accessed | tf_op | source)
XLA Modules:
  0.0 47.0 jit_solution(14707358061434140226)
XLA Ops:
  0.6 1.8 %pack.1 = (f32[7,16,128]{2,1,0:T(8,128)}, f32[7,16,128]{2,1,0:T(8,128)}) custom-call(f32[16,16,128]{2,1,0:T(8,128)} %r_ref.5, f32[16,16,128]{2,1,0:T(8,128)} %d_ref.3, f32[16,16,128]{2,1,0:T(8,128)} %h_ref.3), custom_call_target="tpu_custom_call" | custom-call | tf_op jit(solution)/shard_map/pack/pallas_call | solution.py:216
  2.4 3.0 %collective-permute-start.1 = (f32[7,16,128]{2,1,0:T(8,128)}, f32[7,16,128]{2,1,0:T(8,128)S(1)}, u32[]{:S(2)}, u32[]{:S(2)}) collective-permute-start(f32[7,16,128]{2,1,0:T(8,128)} %get-tuple-element.14.east_own), channel_id=1, source_target_pairs={{0,4},{4,8},{8,12},{12,16},{16,20},{20,24},{24,28},{28,0},{1,5},{5... | collective-permute-start | bytes 172040 | tf_op jit(solution)/shard_map/ppermute | solution.py:224
  5.4 3.0 %collective-permute-start = (f32[7,16,128]{2,1,0:T(8,128)}, f32[7,16,128]{2,1,0:T(8,128)S(1)}, u32[]{:S(2)}, u32[]{:S(2)}) collective-permute-start(f32[7,16,128]{2,1,0:T(8,128)} %get-tuple-element.15.west_own), channel_id=1, source_target_pairs={{4,0},{8,4},{12,8},{16,12},{20,16},{24,20},{28,24},{0,28},{5,1},{9... | collective-permute-start | bytes 172040 | tf_op jit(solution)/shard_map/ppermute | solution.py:225
  8.4 2.4 %collective-permute-done.1.west_ref = f32[7,16,128]{2,1,0:T(8,128)S(1)} collective-permute-done((f32[7,16,128]{2,1,0:T(8,128)}, f32[7,16,128]{2,1,0:T(8,128)S(1)}, u32[]{:S(2)}, u32[]{:S(2)}) %collective-permute-start.1) | collective-permute-done | bytes 57376 | tf_op jit(solution)/shard_map/ppermute | solution.py:224
  10.8 0.0 copy-start.2
  10.8 0.2 collective-permute-done.east_ref
  11.0 0.4 copy-done.2
  11.4 0.0 copy-start.3
  11.4 0.6 %copy-done.3 = f32[7,16,128]{2,1,0:T(8,128)} copy-done((f32[7,16,128]{2,1,0:T(8,128)}, f32[7,16,128]{2,1,0:T(8,128)S(1)}, u32[]{:S(2)}) %copy-start.3) | copy-done | bytes 57368
  12.0 2.0 %widen.1 = (f32[16,24,128]{2,1,0:T(8,128)}, f32[16,24,128]{2,1,0:T(8,128)}, f32[16,24,128]{2,1,0:T(8,128)}, f32[7,24,128]{2,1,0:T(8,128)}, f32[7,24,128]{2,1,0:T(8,128)}, /*index=5*/f32[11,16,128]{2,1,0:T(8,128)}) custom-call(f32[16,16,128]{2,1,0:T(8,128)} %r_ref.5, f32[16,16,128]{2,1,0:T(8,128)} %d_ref.3, f32[16,16,128]{2,1,0:T(8,128)} %h_ref.3, ...), custom_call_target="tpu_custom_call" | custom-call | tf_op jit(solution)/shard_map/widen/pallas_call | solution.py:226
  14.1 1.3 %collective-permute-start.2 = (f32[7,24,128]{2,1,0:T(8,128)}, f32[7,24,128]{2,1,0:T(8,128)S(1)}, u32[]{:S(2)}, u32[]{:S(2)}) collective-permute-start(f32[7,24,128]{2,1,0:T(8,128)} %get-tuple-element.19), channel_id=1, source_target_pairs={{0,1},{1,2},{2,3},{4,5},{5,6},{6,7},{8,9},{9,10},{10,11},{12,13},{... | collective-permute-start | bytes 258056 | tf_op jit(solution)/shard_map/ppermute | solution.py:234
  15.4 1.3 %collective-permute-start.3 = (f32[7,24,128]{2,1,0:T(8,128)}, f32[7,24,128]{2,1,0:T(8,128)S(1)}, u32[]{:S(2)}, u32[]{:S(2)}) collective-permute-start(f32[7,24,128]{2,1,0:T(8,128)} %get-tuple-element.20), channel_id=1, source_target_pairs={{1,0},{2,1},{3,2},{5,4},{6,5},{7,6},{9,8},{10,9},{11,10},{13,12},{... | collective-permute-start | bytes 258056 | tf_op jit(solution)/shard_map/ppermute | solution.py:235
  16.7 10.8 %all-gather = f32[44,16,128]{2,1,0:T(8,128)} all-gather(f32[11,16,128]{2,1,0:T(8,128)} %get-tuple-element.21), channel_id=2, replica_groups=mesh['gx'=8,'gy'=4] {'gy'}, dimensions={0}, use_global_device_ids=true | all-gather | bytes 450560 | tf_op jit(solution)/shard_map/all_gather | solution.py:236
  27.4 0.0 collective-permute-done.2.before
  27.4 0.0 copy-start
  27.4 0.0 collective-permute-done.3.after
  27.4 0.0 copy-start.1
  27.5 0.6 %copy-done = f32[7,24,128]{2,1,0:T(8,128)} copy-done((f32[7,24,128]{2,1,0:T(8,128)}, f32[7,24,128]{2,1,0:T(8,128)S(1)}, u32[]{:S(2)}) %copy-start) | copy-done | bytes 86040
  28.1 0.0 copy-done.1
  28.1 4.8 %krylov.1 = (f32[3,16,16,128]{3,2,1,0:T(8,128)}, f32[3,16,16,128]{3,2,1,0:T(8,128)}, f32[32,1,128]{2,1,0:T(1,128)}) custom-call(s32[2,64]{1,0:T(2,128)} %edges.1, f32[16,24,128]{2,1,0:T(8,128)} %get-tuple-element.16.rw_ref, f32[16,24,128]{2,1,0:T(8,128)} %get-tuple-element.17.dw_ref, f32[16,24,128]{2,1,0:T(8,128)} %get-tuple-element.18.hw_ref, ...), custom_call_target="tpu_custom_call" | custom-call | tf_op jit(solution)/shard_map/krylov/pallas_call | solution.py:238
  32.9 11.9 %all_to_all.5.parts = f32[32,1,128]{2,1,0:T(1,128)} all-to-all(f32[32,1,128]{2,1,0:T(1,128)} %get-tuple-element.22), channel_id=1, replica_groups=mesh['gx'=8,'gy'=4] {'gx','gy'}, dimensions={0} | all-to-all | bytes 32768 | tf_op jit(solution)/shard_map/all_to_all | solution.py:248
  44.8 2.2 %combine.1 = (f32[16,16,128]{2,1,0:T(8,128)}, f32[16,16,128]{2,1,0:T(8,128)}, f32[3]{0:T(128)}) custom-call(f32[32,1,128]{2,1,0:T(1,128)} %all_to_all.5.parts, f32[16,16,128]{2,1,0:T(8,128)} %r_ref.5, f32[3,16,16,128]{3,2,1,0:T(8,128)} %get-tuple-element.23.zs_ref, f32[3,16,16,128]{3,2,1,0:T(8,128)} %get-tuple-element.24.ws_ref), custom_call_target="tpu_custom_call" | custom-call | tf_op jit(solution)/shard_map/combine/pallas_call | solution.py:249
Async XLA Ops:
  2.4 8.4 %collective-permute-start.1 = (f32[7,16,128]{2,1,0:T(8,128)}, f32[7,16,128]{2,1,0:T(8,128)S(1)}, u32[]{:S(2)}, u32[]{:S(2)}) collective-permute-start(f32[7,16,128]{2,1,0:T(8,128)} %get-tuple-element.14.east_own), channel_id=1, source_target_pairs={{0,4},{4,8},{8,12},{12,16},{16,20},{20,24},{24,28},{28,0},{1,5},{5... | collective-permute-start | bytes 172040 | tf_op jit(solution)/shard_map/ppermute | solution.py:224
  5.4 5.6 %collective-permute-start = (f32[7,16,128]{2,1,0:T(8,128)}, f32[7,16,128]{2,1,0:T(8,128)S(1)}, u32[]{:S(2)}, u32[]{:S(2)}) collective-permute-start(f32[7,16,128]{2,1,0:T(8,128)} %get-tuple-element.15.west_own), channel_id=1, source_target_pairs={{4,0},{8,4},{12,8},{16,12},{20,16},{24,20},{28,24},{0,28},{5,1},{9... | collective-permute-start | bytes 172040 | tf_op jit(solution)/shard_map/ppermute | solution.py:225
  10.8 0.6 %copy-start.2 = (f32[7,16,128]{2,1,0:T(8,128)}, f32[7,16,128]{2,1,0:T(8,128)S(1)}, u32[]{:S(2)}) copy-start(f32[7,16,128]{2,1,0:T(8,128)S(1)} %collective-permute-done.1.west_ref) | copy-start | bytes 172036
  11.4 0.6 %copy-start.3 = (f32[7,16,128]{2,1,0:T(8,128)}, f32[7,16,128]{2,1,0:T(8,128)S(1)}, u32[]{:S(2)}) copy-start(f32[7,16,128]{2,1,0:T(8,128)S(1)} %collective-permute-done.east_ref) | copy-start | bytes 172036
  14.1 13.4 %collective-permute-start.2 = (f32[7,24,128]{2,1,0:T(8,128)}, f32[7,24,128]{2,1,0:T(8,128)S(1)}, u32[]{:S(2)}, u32[]{:S(2)}) collective-permute-start(f32[7,24,128]{2,1,0:T(8,128)} %get-tuple-element.19), channel_id=1, source_target_pairs={{0,1},{1,2},{2,3},{4,5},{5,6},{6,7},{8,9},{9,10},{10,11},{12,13},{... | collective-permute-start | bytes 258056 | tf_op jit(solution)/shard_map/ppermute | solution.py:234
  15.4 12.1 %collective-permute-start.3 = (f32[7,24,128]{2,1,0:T(8,128)}, f32[7,24,128]{2,1,0:T(8,128)S(1)}, u32[]{:S(2)}, u32[]{:S(2)}) collective-permute-start(f32[7,24,128]{2,1,0:T(8,128)} %get-tuple-element.20), channel_id=1, source_target_pairs={{1,0},{2,1},{3,2},{5,4},{6,5},{7,6},{9,8},{10,9},{11,10},{13,12},{... | collective-permute-start | bytes 258056 | tf_op jit(solution)/shard_map/ppermute | solution.py:235
  27.4 0.6 %copy-start = (f32[7,24,128]{2,1,0:T(8,128)}, f32[7,24,128]{2,1,0:T(8,128)S(1)}, u32[]{:S(2)}) copy-start(f32[7,24,128]{2,1,0:T(8,128)S(1)} %collective-permute-done.2.before) | copy-start | bytes 258052
  27.4 0.7 %copy-start.1 = (f32[7,24,128]{2,1,0:T(8,128)}, f32[7,24,128]{2,1,0:T(8,128)S(1)}, u32[]{:S(2)}) copy-start(f32[7,24,128]{2,1,0:T(8,128)S(1)} %collective-permute-done.3.after) | copy-start | bytes 258052

commit v3 on v2

--- a/solution.py
+++ b/solution.py
@@ -21,40 +21,40 @@
     return gx, half, east, west
 
 
-def pack_kernel(r_ref, d_ref, h_ref, east_ref, west_ref):
-    cols = r_ref.shape[1]
+def pack_kernel(r_ref, d_ref, h_ref, east_ref, west_ref, last_ref, first_ref):
+    rows, cols, _ = r_ref.shape
     slot = 0
     for ref, depth in ((r_ref, 3), (d_ref, 2), (h_ref, 2)):
+        last_ref[slot : slot + depth] = ref[rows - depth :]
+        first_ref[slot : slot + depth] = ref[:depth]
         for k in range(depth):
             east_ref[slot] = ref[:, cols - 1 - k, :]
             west_ref[slot] = ref[:, k, :]
             slot += 1
 
 
-def widen_kernel(r_ref, d_ref, h_ref, east_own, west_own, east_ref, west_ref,
-                 rw_ref, dw_ref, hw_ref, last_ref, first_ref, strip_ref, *, n_gx):
-    rows, cols, lev = r_ref.shape
+CORNER = ((0, 0), (1, 0), (0, 1), (3, 0), (5, 0))
+
+
+def strip_kernel(east_own, west_own, east_ref, west_ref, strip_ref, *, n_gx):
+    rows = east_ref.shape[1]
     _, _, seam_east, _ = position(n_gx)
-    slot = 0
-    for ref, wide, depth in ((r_ref, rw_ref, 3), (d_ref, dw_ref, 2), (h_ref, hw_ref, 2)):
-        wide[:, :cols, :] = ref[...]
-        wide[:, cols:, :] = jnp.zeros((rows, PAD, lev), jnp.float32)
-        for k in range(depth):
-            wide[:, cols + k, :] = east_ref[slot + k]
-            wide[:, cols + PAD - 1 - k, :] = west_ref[slot + k]
-        last_ref[slot : slot + depth] = wide[rows - depth :]
-        first_ref[slot : slot + depth] = wide[:depth]
-        slot += depth
     for place, k in enumerate((0, 1, 3, 5)):
         strip_ref[place] = jnp.where(seam_east, east_own[k], west_own[k])
     for k in range(7):
         strip_ref[4 + k] = jnp.where(seam_east, east_ref[k], west_ref[k])
-
-
-def krylov_kernel(edges, rw_ref, dw_ref, hw_ref, before, after, ag, vert_ref, pc_ref,
-                  zs_ref, ws_ref, gram_ref, n0_ref, o0_ref, gath_ref, cross_ref, halo_ref, *, n_gx):
-    rows, wide, lev = rw_ref.shape
-    cols = wide - PAD
+    for side, ref in enumerate((east_ref, west_ref)):
+        strip_ref[11 + side] = jnp.zeros_like(strip_ref[11 + side])
+        for j, (slot, row) in enumerate(CORNER):
+            strip_ref[11 + side, pl.ds(j, 1), :] = ref[slot, pl.ds(row, 1), :]
+            strip_ref[11 + side, pl.ds(5 + j, 1), :] = ref[slot, pl.ds(rows - 1 - row, 1), :]
+
+
+def krylov_kernel(edges, r_ref, d_ref, h_ref, east_ref, west_ref, before, after, ag, vert_ref, pc_ref,
+                  zs_ref, ws_ref, gram_ref, n0_ref, o0_ref, gath_ref, cross_ref, halo_ref,
+                  block_ref, dw_ref, hw_ref, *, n_gx):
+    rows, cols, lev = r_ref.shape
+    wide = cols + PAD
     n_gy = ag.shape[0]
     high = rows * n_gy
     first = lax.axis_index("gy") * rows
@@ -104,9 +104,31 @@
             return 0
         lax.fori_loop(0, high, body, 0, unroll=16)
 
-    block = jnp.concatenate([before[0:3], rw_ref[...], after[0:3]], 0)
-    d = jnp.concatenate([before[3:5], dw_ref[...], after[3:5]], 0)
-    h = jnp.concatenate([before[5:7], hw_ref[...], after[5:7]], 0)
+    gy = lax.axis_index("gy")
+    sources = ((r_ref, block_ref, 3, 0), (d_ref, dw_ref, 2, 3), (h_ref, hw_ref, 2, 5))
+    for ref, target, depth, slot in sources:
+        target[:, cols:, :] = jnp.zeros((rows + 2 * depth, PAD, lev), jnp.float32)
+        target[:depth, :cols, :] = before[slot : slot + depth]
+        target[depth : depth + rows, :cols, :] = ref[...]
+        target[depth + rows :, :cols, :] = after[slot : slot + depth]
+        for k in range(depth):
+            target[depth : depth + rows, cols + k, :] = east_ref[slot + k]
+            target[depth : depth + rows, wide - 1 - k, :] = west_ref[slot + k]
+    above = jnp.minimum(gy + 1, n_gy - 1)
+    below = jnp.maximum(gy - 1, 0)
+    places = ((block_ref, 3), (block_ref, 3), (block_ref, 3), (dw_ref, 2), (hw_ref, 2))
+    for side in range(2):
+        high_corner = jnp.where(gy + 1 < n_gy, ag[above, 11 + side], 0.0)
+        low_corner = jnp.where(gy > 0, ag[below, 11 + side], 0.0)
+        for j, (target, depth) in enumerate(places):
+            slot, row = CORNER[j]
+            step = slot if slot < 3 else 0
+            col = cols + step if side == 0 else wide - 1 - step
+            target[depth + rows + row, pl.ds(col, 1), :] = high_corner[j : j + 1]
+            target[depth - 1 - row, pl.ds(col, 1), :] = low_corner[5 + j : 6 + j]
+    block = block_ref[...]
+    d = dw_ref[...]
+    h = hw_ref[...]
 
     own = mul(jnp.stack([strip(0), strip(1)], 0), m_own)
     near = mul(jnp.stack([strip(4), strip(5), strip(6)], 0), m_near)
@@ -140,7 +162,7 @@
     w2 = block_apply(z, d[2:-2], h[2:-2], 0)[:, :cols]
     ws_ref[2] = w2
 
-    vectors = (rw_ref[:, :cols, :], w0, w1, w2)
+    vectors = (r_ref[...], w0, w1, w2)
     lane = lax.broadcasted_iota(jnp.int32, (1, lev), 1)
     row = jnp.zeros((1, lev), jnp.float32)
     count = 0
@@ -206,44 +228,49 @@
     n_gx = lax.axis_size("gx")
     n_gy = lax.axis_size("gy")
     n_dev = n_gx * n_gy
-    assert n_gx >= 4 and cols >= 3 and cols % 8 == 0
+    assert n_gx >= 4 and rows >= 10 and cols % 8 == 0
     high = rows * n_gy
     wide = cols + PAD
     cells = float(rows * cols * levels * n_dev)
     f32 = jnp.float32
     shaped = lambda *shape: jax.ShapeDtypeStruct(shape, f32)
 
-    east_pack, west_pack = pl.pallas_call(
+    east_pack, west_pack, last, initial = pl.pallas_call(
         pack_kernel,
-        out_shape=(shaped(7, rows, levels),) * 2,
+        out_shape=(shaped(7, rows, levels),) * 2 + (shaped(7, cols, levels),) * 2,
         in_specs=[VM] * 3,
-        out_specs=(VM,) * 2,
+        out_specs=(VM,) * 4,
         name="pack",
     )(right_side, diagonal, horizontal)
     ring = [(i, (i + 1) % n_gx) for i in range(n_gx)]
     from_west = lax.ppermute(east_pack, "gx", ring)
     from_east = lax.ppermute(west_pack, "gx", [(j, i) for i, j in ring])
-    rw, dw, hw, last, initial, strips = pl.pallas_call(
-        functools.partial(widen_kernel, n_gx=n_gx),
-        out_shape=(shaped(rows, wide, levels),) * 3 + (shaped(7, wide, levels),) * 2 + (shaped(11, rows, levels),),
-        in_specs=[VM] * 7,
-        out_specs=(VM,) * 6,
-        name="widen",
-    )(right_side, diagonal, horizontal, east_pack, west_pack, from_east, from_west)
     line = [(i, i + 1) for i in range(n_gy - 1)]
     before = lax.ppermute(last, "gy", line)
     after = lax.ppermute(initial, "gy", [(j, i) for i, j in line])
+    strips = pl.pallas_call(
+        functools.partial(strip_kernel, n_gx=n_gx),
+        out_shape=shaped(13, rows, levels),
+        in_specs=[VM] * 4,
+        out_specs=VM,
+        name="strips",
+    )(east_pack, west_pack, from_east, from_west)
     ag = lax.all_gather(strips, "gy")
 
     zs, ws, gram = pl.pallas_call(
         functools.partial(krylov_kernel, n_gx=n_gx),
         out_shape=(shaped(3, rows, cols, levels), shaped(3, rows, cols, levels), shaped(n_dev, 1, levels)),
-        in_specs=[SM] + [VM] * 8,
+        in_specs=[SM] + [VM] * 10,
         out_specs=(VM, VM, VM),
         scratch_shapes=[pltpu.VMEM((high, levels), f32)] * 4
-        + [pltpu.VMEM((rows + 4, 1, levels), f32)],
+        + [
+            pltpu.VMEM((rows + 4, 1, levels), f32),
+            pltpu.VMEM((rows + 6, wide, levels), f32),
+            pltpu.VMEM((rows + 4, wide, levels), f32),
+            pltpu.VMEM((rows + 4, wide, levels), f32),
+        ],
         name="krylov",
-    )(edge_rows, rw, dw, hw, before, after, ag, vertical[None], precond)
+    )(edge_rows, right_side, diagonal, horizontal, from_east, from_west, before, after, ag, vertical[None], precond)
 
     parts = lax.all_to_all(gram, ("gx", "gy"), 0, 0)
     return pl.pallas_call(

time: 47.4 us -> 45.4 us (0.958)
  blocking collectives: 22.7 us -> 19.6 us
  waiting for transfers between devices: 2.58 us -> 4.31 us
    ppermute x1, starting transfers between devices: 3.04 us -> 6.03 us  [on_device(): from_east = lax.ppermute(west_pack, 'gx', [(j, i) for i, j in ring])]
    ppermute x1, starting transfers between devices: 3 us -> 0.01 us  [on_device(): from_west = lax.ppermute(east_pack, 'gx', ring)]
    all_gather x1, blocking collectives: 10.8 us -> 7.82 us  [on_device(): ag = lax.all_gather(strips, 'gy')]
    ppermute x1, waiting for transfers between devices: 2.36 us -> 4.3 us  [on_device(): from_west = lax.ppermute(east_pack, 'gx', ring)]
  transfers between devices with their start and end apart: 4 -> 4, of which waited for: 2 -> 1; matrix products, arithmetic and copies ran while one was open for 0% -> 0% of each run, Pallas kernels for 0% -> 3%
where the time goes in v3:
time: 45.4 us; the launch traced here: 45.1 us
  blocking collectives  19.6 us (43%)
  Pallas kernels  10.4 us (23%)
  starting transfers between devices  8.78 us (19%)
  waiting for transfers between devices  4.31 us (9%)
  local copies, waits for them, and re-layouts  1.25 us (3%)
  between operations  0.68 us (1%)
    all_to_all x1, blocking collectives, on_device(): parts = lax.all_to_all(gram, ('gx', 'gy'), 0, 0)  11.8 us
    all_gather x1, blocking collectives, on_device(): ag = lax.all_gather(strips, 'gy')  7.82 us
    ppermute x1, starting transfers between devices, on_device(): from_east = lax.ppermute(west_pack, 'gx', [(j, i) for i, j in ring])  6.03 us
    pallas_call x1, Pallas kernels, on_device(): pl.pallas_call(functools.partial(krylov_kernel, n_gx=n_gx), out_shape=(sh...  4.86 us
    ppermute x1, waiting for transfers between devices, on_device(): from_west = lax.ppermute(east_pack, 'gx', ring)  4.3 us
    pallas_call x1, Pallas kernels, on_device(): pl.pallas_call(functools.partial(combine_kernel, cells=cells), out_shape=...  2.25 us
    pallas_call x1, Pallas kernels, on_device(): pl.pallas_call(pack_kernel, out_shape=(shaped(7, rows, levels),) * 2 + (s...  1.78 us
    pallas_call x1, Pallas kernels, on_device(): pl.pallas_call(functools.partial(strip_kernel, n_gx=n_gx), out_shape=shap...  1.56 us
  transfers between devices with their start and end apart: 4, of which 1 were waited for; matrix products, arithmetic and copies ran while one was open for 0% of the time, Pallas kernels for 3%

profile of v3, /device:TPU:0, one launch (start us, length us, event | category | flops | bytes accessed | tf_op | source)
XLA Modules:
  0.0 45.1 jit_solution(18144092030984244996)
XLA Ops:
  0.6 1.8 %pack.1 = (f32[7,16,128]{2,1,0:T(8,128)}, f32[7,16,128]{2,1,0:T(8,128)}, f32[7,16,128]{2,1,0:T(8,128)}, f32[7,16,128]{2,1,0:T(8,128)}) custom-call(f32[16,16,128]{2,1,0:T(8,128)} %r_ref.5, f32[16,16,128]{2,1,0:T(8,128)} %d_ref.3, f32[16,16,128]{2,1,0:T(8,128)} %h_ref.3), custom_call_target="tpu_custom_call" | custom-call | tf_op jit(solution)/shard_map/pack/pallas_call | solution.py:238
  2.4 6.0 %collective-permute-start = (f32[7,16,128]{2,1,0:T(8,128)}, f32[7,16,128]{2,1,0:T(8,128)S(1)}, u32[]{:S(2)}, u32[]{:S(2)}) collective-permute-start(f32[7,16,128]{2,1,0:T(8,128)} %get-tuple-element.10.west_own), channel_id=1, source_target_pairs={{4,0},{8,4},{12,8},{16,12},{20,16},{24,20},{28,24},{0,28},{5,1},{9... | collective-permute-start | bytes 172040 | tf_op jit(solution)/shard_map/ppermute | solution.py:247
  8.4 0.0 collective-permute-start.1
  8.4 1.4 %collective-permute-start.2 = (f32[7,16,128]{2,1,0:T(8,128)}, f32[7,16,128]{2,1,0:T(8,128)S(1)}, u32[]{:S(2)}, u32[]{:S(2)}) collective-permute-start(f32[7,16,128]{2,1,0:T(8,128)} %get-tuple-element.12), channel_id=1, source_target_pairs={{0,1},{1,2},{2,3},{4,5},{5,6},{6,7},{8,9},{9,10},{10,11},{12,13},{... | collective-permute-start | bytes 172040 | tf_op jit(solution)/shard_map/ppermute | solution.py:249
  9.9 1.3 %collective-permute-start.3 = (f32[7,16,128]{2,1,0:T(8,128)}, f32[7,16,128]{2,1,0:T(8,128)S(1)}, u32[]{:S(2)}, u32[]{:S(2)}) collective-permute-start(f32[7,16,128]{2,1,0:T(8,128)} %get-tuple-element.13), channel_id=1, source_target_pairs={{1,0},{2,1},{3,2},{5,4},{6,5},{7,6},{9,8},{10,9},{11,10},{13,12},{... | collective-permute-start | bytes 172040 | tf_op jit(solution)/shard_map/ppermute | solution.py:250
  11.2 0.0 collective-permute-done.east_ref
  11.2 0.0 copy-start
  11.2 4.3 %collective-permute-done.1.west_ref = f32[7,16,128]{2,1,0:T(8,128)S(1)} collective-permute-done((f32[7,16,128]{2,1,0:T(8,128)}, f32[7,16,128]{2,1,0:T(8,128)S(1)}, u32[]{:S(2)}, u32[]{:S(2)}) %collective-permute-start.1) | collective-permute-done | bytes 57376 | tf_op jit(solution)/shard_map/ppermute | solution.py:246
  15.5 0.0 copy-done
  15.5 0.0 copy-start.1
  15.5 0.6 %copy-done.1 = f32[7,16,128]{2,1,0:T(8,128)} copy-done((f32[7,16,128]{2,1,0:T(8,128)}, f32[7,16,128]{2,1,0:T(8,128)S(1)}, u32[]{:S(2)}) %copy-start.1) | copy-done | bytes 57368
  16.1 1.6 %strips.1 = f32[13,16,128]{2,1,0:T(8,128)} custom-call(f32[7,16,128]{2,1,0:T(8,128)} %get-tuple-element.11.east_own, f32[7,16,128]{2,1,0:T(8,128)} %get-tuple-element.10.west_own, f32[7,16,128]{2,1,0:T(8,128)} %copy-done, f32[7,16,128]{2,1,0:T(8,128)} %copy-done.1), custom_call_target="tpu_custom_call" | custom-call | tf_op jit(solution)/shard_map/strips/pallas_call | solution.py:251
  17.7 7.8 %all-gather = f32[52,16,128]{2,1,0:T(8,128)} all-gather(f32[13,16,128]{2,1,0:T(8,128)} %strips.1), channel_id=2, replica_groups=mesh['gx'=8,'gy'=4] {'gy'}, dimensions={0}, use_global_device_ids=true | all-gather | bytes 532480 | tf_op jit(solution)/shard_map/all_gather | solution.py:258
  25.5 0.0 collective-permute-done.2.before
  25.5 0.0 copy-start.2
  25.5 0.0 collective-permute-done.3.after
  25.5 0.0 copy-start.3
  25.6 0.6 %copy-done.2 = f32[7,16,128]{2,1,0:T(8,128)} copy-done((f32[7,16,128]{2,1,0:T(8,128)}, f32[7,16,128]{2,1,0:T(8,128)S(1)}, u32[]{:S(2)}) %copy-start.2) | copy-done | bytes 57368
  26.2 0.0 copy-done.3
  26.2 4.9 %krylov.1 = (f32[3,16,16,128]{3,2,1,0:T(8,128)}, f32[3,16,16,128]{3,2,1,0:T(8,128)}, f32[32,1,128]{2,1,0:T(1,128)}) custom-call(s32[2,64]{1,0:T(2,128)} %edges.1, f32[16,16,128]{2,1,0:T(8,128)} %r_ref.5, f32[16,16,128]{2,1,0:T(8,128)} %d_ref.3, f32[16,16,128]{2,1,0:T(8,128)} %h_ref.3, f32[7,16,128]{2,1,0:T(8,128)} %copy-done, f32[7,16,128]{2,1,0:T(8,128)} %copy-done.1, ...), custom_call_target="tpu_custom_call" | custom-call | tf_op jit(solution)/shard_map/krylov/pallas_call | solution.py:260
  31.0 11.8 %all_to_all.5.parts = f32[32,1,128]{2,1,0:T(1,128)} all-to-all(f32[32,1,128]{2,1,0:T(1,128)} %get-tuple-element.14), channel_id=1, replica_groups=mesh['gx'=8,'gy'=4] {'gx','gy'}, dimensions={0} | all-to-all | bytes 32768 | tf_op jit(solution)/shard_map/all_to_all | solution.py:275
  42.8 2.2 %combine.1 = (f32[16,16,128]{2,1,0:T(8,128)}, f32[16,16,128]{2,1,0:T(8,128)}, f32[3]{0:T(128)}) custom-call(f32[32,1,128]{2,1,0:T(1,128)} %all_to_all.5.parts, f32[16,16,128]{2,1,0:T(8,128)} %r_ref.5, f32[3,16,16,128]{3,2,1,0:T(8,128)} %get-tuple-element.15.zs_ref, f32[3,16,16,128]{3,2,1,0:T(8,128)} %get-tuple-element.16.ws_ref), custom_call_target="tpu_custom_call" | custom-call | tf_op jit(solution)/shard_map/combine/pallas_call | solution.py:276
Async XLA Ops:
  2.4 8.8 %collective-permute-start = (f32[7,16,128]{2,1,0:T(8,128)}, f32[7,16,128]{2,1,0:T(8,128)S(1)}, u32[]{:S(2)}, u32[]{:S(2)}) collective-permute-start(f32[7,16,128]{2,1,0:T(8,128)} %get-tuple-element.10.west_own), channel_id=1, source_target_pairs={{4,0},{8,4},{12,8},{16,12},{20,16},{24,20},{28,24},{0,28},{5,1},{9... | collective-permute-start | bytes 172040 | tf_op jit(solution)/shard_map/ppermute | solution.py:247
  8.4 7.1 %collective-permute-start.1 = (f32[7,16,128]{2,1,0:T(8,128)}, f32[7,16,128]{2,1,0:T(8,128)S(1)}, u32[]{:S(2)}, u32[]{:S(2)}) collective-permute-start(f32[7,16,128]{2,1,0:T(8,128)} %get-tuple-element.11.east_own), channel_id=1, source_target_pairs={{0,4},{4,8},{8,12},{12,16},{16,20},{20,24},{24,28},{28,0},{1,5},{5... | collective-permute-start | bytes 172040 | tf_op jit(solution)/shard_map/ppermute | solution.py:246
  8.4 17.1 %collective-permute-start.2 = (f32[7,16,128]{2,1,0:T(8,128)}, f32[7,16,128]{2,1,0:T(8,128)S(1)}, u32[]{:S(2)}, u32[]{:S(2)}) collective-permute-start(f32[7,16,128]{2,1,0:T(8,128)} %get-tuple-element.12), channel_id=1, source_target_pairs={{0,1},{1,2},{2,3},{4,5},{5,6},{6,7},{8,9},{9,10},{10,11},{12,13},{... | collective-permute-start | bytes 172040 | tf_op jit(solution)/shard_map/ppermute | solution.py:249
  9.9 15.6 %collective-permute-start.3 = (f32[7,16,128]{2,1,0:T(8,128)}, f32[7,16,128]{2,1,0:T(8,128)S(1)}, u32[]{:S(2)}, u32[]{:S(2)}) collective-permute-start(f32[7,16,128]{2,1,0:T(8,128)} %get-tuple-element.13), channel_id=1, source_target_pairs={{1,0},{2,1},{3,2},{5,4},{6,5},{7,6},{9,8},{10,9},{11,10},{13,12},{... | collective-permute-start | bytes 172040 | tf_op jit(solution)/shard_map/ppermute | solution.py:250
  11.2 4.3 %copy-start = (f32[7,16,128]{2,1,0:T(8,128)}, f32[7,16,128]{2,1,0:T(8,128)S(1)}, u32[]{:S(2)}) copy-start(f32[7,16,128]{2,1,0:T(8,128)S(1)} %collective-permute-done.east_ref) | copy-start | bytes 172036
  15.5 0.6 %copy-start.1 = (f32[7,16,128]{2,1,0:T(8,128)}, f32[7,16,128]{2,1,0:T(8,128)S(1)}, u32[]{:S(2)}) copy-start(f32[7,16,128]{2,1,0:T(8,128)S(1)} %collective-permute-done.1.west_ref) | copy-start | bytes 172036
  25.5 0.6 %copy-start.2 = (f32[7,16,128]{2,1,0:T(8,128)}, f32[7,16,128]{2,1,0:T(8,128)S(1)}, u32[]{:S(2)}) copy-start(f32[7,16,128]{2,1,0:T(8,128)S(1)} %collective-permute-done.2.before) | copy-start | bytes 172036
  25.5 0.6 %copy-start.3 = (f32[7,16,128]{2,1,0:T(8,128)}, f32[7,16,128]{2,1,0:T(8,128)S(1)}, u32[]{:S(2)}) copy-start(f32[7,16,128]{2,1,0:T(8,128)S(1)} %collective-permute-done.3.after) | copy-start | bytes 172036

commit v4 on v3

--- a/solution.py
+++ b/solution.py
@@ -8,6 +8,7 @@
 from jax.sharding import PartitionSpec as P
 
 PAD = 8
+HELD_LIMIT = 2**21 + 2**19
 HI = lax.Precision.HIGHEST
 VM = pl.BlockSpec(memory_space=pltpu.VMEM)
 SM = pl.BlockSpec(memory_space=pltpu.SMEM)
@@ -233,7 +234,13 @@
     wide = cols + PAD
     cells = float(rows * cols * levels * n_dev)
     f32 = jnp.float32
-    shaped = lambda *shape: jax.ShapeDtypeStruct(shape, f32)
+    held = 4 * levels * (6 * rows * cols + 13 * rows * (n_gy + 1) + 28 * (rows + cols))
+    if held <= HELD_LIMIT:
+        near = lambda x: pltpu.with_memory_space_constraint(x, pltpu.VMEM)
+        shaped = lambda *shape: pltpu.VMEM(shape, f32)
+    else:
+        near = lambda x: x
+        shaped = lambda *shape: jax.ShapeDtypeStruct(shape, f32)
 
     east_pack, west_pack, last, initial = pl.pallas_call(
         pack_kernel,
@@ -254,7 +261,7 @@
         in_specs=[VM] * 4,
         out_specs=VM,
         name="strips",
-    )(east_pack, west_pack, from_east, from_west)
+    )(*map(near, (east_pack, west_pack, from_east, from_west)))
     ag = lax.all_gather(strips, "gy")
 
     zs, ws, gram = pl.pallas_call(
@@ -270,7 +277,7 @@
             pltpu.VMEM((rows + 4, wide, levels), f32),
         ],
         name="krylov",
-    )(edge_rows, right_side, diagonal, horizontal, from_east, from_west, before, after, ag, vertical[None], precond)
+    )(edge_rows, right_side, diagonal, horizontal, *map(near, (from_east, from_west, before, after, ag)), vertical[None], precond)
 
     parts = lax.all_to_all(gram, ("gx", "gy"), 0, 0)
     return pl.pallas_call(
@@ -283,7 +290,7 @@
         in_specs=[VM] * 4,
         out_specs=(VM, VM, SM),
         name="combine",
-    )(parts, right_side, zs, ws)
+    )(near(parts), right_side, near(zs), near(ws))
 
 
 def solution(mesh):

time: 45.4 us -> 38.9 us (0.86)
  Pallas kernels: 10.4 us -> 7.09 us
  blocking collectives: 19.6 us -> 17.9 us
  local copies, waits for them, and re-layouts: 1.25 us -> 0 us
    pallas_call x1, Pallas kernels: 1.56 us -> 0.03 us  [on_device(): pl.pallas_call(functools.partial(strip_kernel, n_gx=n_gx), out_shape=shap...]
    unnamed x8 -> x0, local copies, waits for them, and re-layouts: 1.25 us -> none
    all_gather x1, blocking collectives: 7.82 us -> 6.64 us  [on_device(): ag = lax.all_gather(strips, 'gy')]
    pallas_call x1, Pallas kernels: 4.86 us -> 4.02 us  [on_device(): pl.pallas_call(functools.partial(krylov_kernel, n_gx=n_gx), out_shape=(sh...]
    pallas_call x1, Pallas kernels: 1.78 us -> 1.1 us  [on_device(): pl.pallas_call(pack_kernel, out_shape=(shaped(7, rows, levels),) * 2 + (s...]
    all_to_all x1, blocking collectives: 11.8 us -> 11.3 us  [on_device(): parts = lax.all_to_all(gram, ('gx', 'gy'), 0, 0)]
  transfers between devices with their start and end apart: 4 -> 4, of which waited for: 1 -> 1; matrix products, arithmetic and copies ran while one was open for 0% -> 0% of each run, Pallas kernels for 3% -> 0%
where the time goes in v4:
time: 38.9 us; the launch traced here: 38.7 us
  blocking collectives  17.9 us (46%)
  starting transfers between devices  8.83 us (23%)
  Pallas kernels  7.09 us (18%)
  waiting for transfers between devices  4.11 us (11%)
  between operations  0.67 us (2%)
    all_to_all x1, blocking collectives, on_device(): parts = lax.all_to_all(gram, ('gx', 'gy'), 0, 0)  11.3 us
    all_gather x1, blocking collectives, on_device(): ag = lax.all_gather(strips, 'gy')  6.64 us
    ppermute x1, starting transfers between devices, on_device(): from_east = lax.ppermute(west_pack, 'gx', [(j, i) for i, j in ring])  6.09 us
    ppermute x1, waiting for transfers between devices, on_device(): from_west = lax.ppermute(east_pack, 'gx', ring)  4.1 us
    pallas_call x1, Pallas kernels, on_device(): pl.pallas_call(functools.partial(krylov_kernel, n_gx=n_gx), out_shape=(sh...  4.02 us
    pallas_call x1, Pallas kernels, on_device(): pl.pallas_call(functools.partial(combine_kernel, cells=cells), out_shape=...  1.94 us
    ppermute x1, starting transfers between devices, on_device(): before = lax.ppermute(last, 'gy', line)  1.45 us
    ppermute x1, starting transfers between devices, on_device(): after = lax.ppermute(initial, 'gy', [(j, i) for i, j in line])  1.29 us
  transfers between devices with their start and end apart: 4, of which 1 were waited for; matrix products, arithmetic and copies ran while one was open for 0% of the time, Pallas kernels for 0%

profile of v4, /device:TPU:0, one launch (start us, length us, event | category | flops | bytes accessed | tf_op | source)
XLA Modules:
  0.0 38.7 jit_solution(11742601976740793940)
XLA Ops:
  0.6 1.1 %pack.1 = (f32[7,16,128]{2,1,0:T(8,128)S(1)}, f32[7,16,128]{2,1,0:T(8,128)S(1)}, f32[7,16,128]{2,1,0:T(8,128)S(1)}, f32[7,16,128]{2,1,0:T(8,128)S(1)}) custom-call(f32[16,16,128]{2,1,0:T(8,128)} %r_ref.5, f32[16,16,128]{2,1,0:T(8,128)} %d_ref.3, f32[16,16,128]{2,1,0:T(8,128)} %h_ref.3), custom_call_target="tpu_custom_call" | custom-call | tf_op jit(solution)/shard_map/pack/pallas_call | solution.py:245
  1.7 6.1 %collective-permute-start = (f32[7,16,128]{2,1,0:T(8,128)S(1)}, f32[7,16,128]{2,1,0:T(8,128)S(1)}, u32[]{:S(2)}, u32[]{:S(2)}) collective-permute-start(f32[7,16,128]{2,1,0:T(8,128)S(1)} %get-tuple-element.10.west_own), channel_id=1, source_target_pairs={{4,0},{8,4},{12,8},{16,12},{20,16},{24,20},{28,24},{0,28},{5,1},{9... | collective-permute-start | bytes 172040 | tf_op jit(solution)/shard_map/ppermute | solution.py:254
  7.8 0.0 collective-permute-start.1
  7.8 1.4 %collective-permute-start.2 = (f32[7,16,128]{2,1,0:T(8,128)S(1)}, f32[7,16,128]{2,1,0:T(8,128)S(1)}, u32[]{:S(2)}, u32[]{:S(2)}) collective-permute-start(f32[7,16,128]{2,1,0:T(8,128)S(1)} %get-tuple-element.12), channel_id=1, source_target_pairs={{0,1},{1,2},{2,3},{4,5},{5,6},{6,7},{8,9},{9,10},{10,11},{12,13},{... | collective-permute-start | bytes 172040 | tf_op jit(solution)/shard_map/ppermute | solution.py:256
  9.3 1.3 %collective-permute-start.3 = (f32[7,16,128]{2,1,0:T(8,128)S(1)}, f32[7,16,128]{2,1,0:T(8,128)S(1)}, u32[]{:S(2)}, u32[]{:S(2)}) collective-permute-start(f32[7,16,128]{2,1,0:T(8,128)S(1)} %get-tuple-element.13), channel_id=1, source_target_pairs={{1,0},{2,1},{3,2},{5,4},{6,5},{7,6},{9,8},{10,9},{11,10},{13,12},{... | collective-permute-start | bytes 172040 | tf_op jit(solution)/shard_map/ppermute | solution.py:257
  10.6 0.0 collective-permute-done.east_ref
  10.6 4.1 %collective-permute-done.1.west_ref = f32[7,16,128]{2,1,0:T(8,128)S(1)} collective-permute-done((f32[7,16,128]{2,1,0:T(8,128)S(1)}, f32[7,16,128]{2,1,0:T(8,128)S(1)}, u32[]{:S(2)}, u32[]{:S(2)}) %collective-permute-start.1) | collective-permute-done | bytes 57376 | tf_op jit(solution)/shard_map/ppermute | solution.py:253
  14.7 6.6 %all-gather = f32[52,16,128]{2,1,0:T(8,128)S(1)} all-gather(f32[13,16,128]{2,1,0:T(8,128)S(1)} %strips.1), channel_id=2, replica_groups=mesh['gx'=8,'gy'=4] {'gy'}, dimensions={0}, use_global_device_ids=true | all-gather | bytes 532480 | tf_op jit(solution)/shard_map/all_gather | solution.py:265
  21.4 0.0 collective-permute-done.2.before
  21.4 0.0 collective-permute-done.3.after
  21.4 4.0 %krylov.1 = (f32[3,16,16,128]{3,2,1,0:T(8,128)S(1)}, f32[3,16,16,128]{3,2,1,0:T(8,128)S(1)}, f32[32,1,128]{2,1,0:T(1,128)S(1)}) custom-call(s32[2,64]{1,0:T(2,128)} %edges.1, f32[16,16,128]{2,1,0:T(8,128)} %r_ref.5, f32[16,16,128]{2,1,0:T(8,128)} %d_ref.3, f32[16,16,128]{2,1,0:T(8,128)} %h_ref.3, f32[7,16,128]{2,1,0:T(8,128)S(1)} %collective-permute-done.east_ref, ...), custom_call_target="tpu_custom_call" | custom-call | tf_op jit(solution)/shard_map/krylov/pallas_call | solution.py:267
  25.4 11.3 %all_to_all.5.parts = f32[32,1,128]{2,1,0:T(1,128)S(1)} all-to-all(f32[32,1,128]{2,1,0:T(1,128)S(1)} %get-tuple-element.14), channel_id=1, replica_groups=mesh['gx'=8,'gy'=4] {'gx','gy'}, dimensions={0} | all-to-all | bytes 32768 | tf_op jit(solution)/shard_map/all_to_all | solution.py:282
  36.7 1.9 %combine.1 = (f32[16,16,128]{2,1,0:T(8,128)}, f32[16,16,128]{2,1,0:T(8,128)}, f32[3]{0:T(128)}) custom-call(f32[32,1,128]{2,1,0:T(1,128)S(1)} %all_to_all.5.parts, f32[16,16,128]{2,1,0:T(8,128)} %r_ref.5, f32[3,16,16,128]{3,2,1,0:T(8,128)S(1)} %get-tuple-element.15.zs_ref, f32[3,16,16,128]{3,2,1,0:T(8,128)S(1)} %get-tuple-element.16.ws_ref), custom_call_target="tpu_custom_call" | custom-call | tf_op jit(solution)/shard_map/combine/pallas_call | solution.py:283
  (1 shorter events, 0.0 us)
Async XLA Ops:
  1.7 8.8 %collective-permute-start = (f32[7,16,128]{2,1,0:T(8,128)S(1)}, f32[7,16,128]{2,1,0:T(8,128)S(1)}, u32[]{:S(2)}, u32[]{:S(2)}) collective-permute-start(f32[7,16,128]{2,1,0:T(8,128)S(1)} %get-tuple-element.10.west_own), channel_id=1, source_target_pairs={{4,0},{8,4},{12,8},{16,12},{20,16},{24,20},{28,24},{0,28},{5,1},{9... | collective-permute-start | bytes 172040 | tf_op jit(solution)/shard_map/ppermute | solution.py:254
  7.8 6.9 %collective-permute-start.1 = (f32[7,16,128]{2,1,0:T(8,128)S(1)}, f32[7,16,128]{2,1,0:T(8,128)S(1)}, u32[]{:S(2)}, u32[]{:S(2)}) collective-permute-start(f32[7,16,128]{2,1,0:T(8,128)S(1)} %get-tuple-element.11.east_own), channel_id=1, source_target_pairs={{0,4},{4,8},{8,12},{12,16},{16,20},{20,24},{24,28},{28,0},{1,5},{5... | collective-permute-start | bytes 172040 | tf_op jit(solution)/shard_map/ppermute | solution.py:253
  7.8 13.5 %collective-permute-start.2 = (f32[7,16,128]{2,1,0:T(8,128)S(1)}, f32[7,16,128]{2,1,0:T(8,128)S(1)}, u32[]{:S(2)}, u32[]{:S(2)}) collective-permute-start(f32[7,16,128]{2,1,0:T(8,128)S(1)} %get-tuple-element.12), channel_id=1, source_target_pairs={{0,1},{1,2},{2,3},{4,5},{5,6},{6,7},{8,9},{9,10},{10,11},{12,13},{... | collective-permute-start | bytes 172040 | tf_op jit(solution)/shard_map/ppermute | solution.py:256
  9.3 12.1 %collective-permute-start.3 = (f32[7,16,128]{2,1,0:T(8,128)S(1)}, f32[7,16,128]{2,1,0:T(8,128)S(1)}, u32[]{:S(2)}, u32[]{:S(2)}) collective-permute-start(f32[7,16,128]{2,1,0:T(8,128)S(1)} %get-tuple-element.13), channel_id=1, source_target_pairs={{1,0},{2,1},{3,2},{5,4},{6,5},{7,6},{9,8},{10,9},{11,10},{13,12},{... | collective-permute-start | bytes 172040 | tf_op jit(solution)/shard_map/ppermute | solution.py:257
